TPU v7x, 512 devices: a whole 4x8x8 slice. The times are simulated.
512 devices in a mesh: ctx: 64 (over z, x, core), tp: 8 (over y).
Axes of the slice: x: 4, y: 8, z: 8, core: 2. Of those that a mesh axis runs over, the one named last changes fastest.
Arguments:
- queries: bfloat16 [16384, 8192], P('ctx', 'tp'), may hold values from -6 to 6
- key_vectors: bfloat16 [16384, 1024], P(('ctx', 'tp')), may hold values from -6 to 6
- value_vectors: bfloat16 [16384, 1024], P(('ctx', 'tp')), may hold values from -6 to 6
- output_gradient: bfloat16 [16384, 8192], P('ctx', 'tp'), may hold values from -6 to 6
- doc_lengths: int32 [32], replicated, may hold values from 1 to 1793, 16384 in all
Outputs:
- attn_output: bfloat16 [16384, 8192], P('ctx', 'tp')
- grad_queries: bfloat16 [16384, 8192], P('ctx', 'tp')
- key_gradient: bfloat16 [16384, 1024], P(('ctx', 'tp'))
- value_gradient: bfloat16 [16384, 1024], P(('ctx', 'tp'))
All inputs are finite; a program needn't handle non-finite values.
Results may differ from a plain program's by a relative error of at most 0.02.
Values may be sent and summed in bfloat16 or wider, within the bound.
A program may use at most 64 MiB of HBM per device.

v0:
```python
import math

import jax
import jax.numpy as jnp
from jax import lax
from jax.sharding import PartitionSpec as P

HEAD_SIZE = 128
WINDOW = 8


def shifted(value, axis, steps):
    count = lax.axis_size(axis)
    leading, last = (max(0, -steps), min(count, count - steps))
    return lax.ppermute(value, axis, [(source, source + steps) for source in range(leading, last)])


def doc_index_of(positions, doc_starts):
    above = (positions[:, None] >= doc_starts[None, :]).astype(jnp.int32)
    return jnp.sum(above, axis=1) - 1


def attend_block(block_q, block_g, key_block, value_block, allowed, score_scale):
    scores = (
        jnp.einsum("thd,kd->htk", block_q, key_block, preferred_element_type=jnp.float32)
        * score_scale
    )
    scores = jnp.where(allowed[None], scores, -1e30)
    row_top = jnp.max(scores, axis=2, keepdims=True)
    row_total = jnp.sum(jnp.exp(scores - row_top), axis=2, keepdims=True)
    log_total = row_top + jnp.log(row_total)
    weights = jnp.exp(scores - log_total)
    weights_low = weights.astype(jnp.bfloat16)
    output = jnp.einsum(
        "htk,kd->thd", weights_low, value_block, preferred_element_type=jnp.float32
    ).astype(jnp.bfloat16)
    row_delta = jnp.sum(output.astype(jnp.float32) * block_g.astype(jnp.float32), axis=2)
    row_delta = jnp.transpose(row_delta)[:, :, None]
    grad_weights = jnp.einsum(
        "thd,kd->htk", block_g, value_block, preferred_element_type=jnp.float32
    )
    grad_scores = (weights * (grad_weights - row_delta) * score_scale).astype(jnp.bfloat16)
    grad_query = jnp.einsum(
        "htk,kd->thd", grad_scores, key_block, preferred_element_type=jnp.float32
    ).astype(jnp.bfloat16)
    grad_key = jnp.einsum("htk,thd->kd", grad_scores, block_q, preferred_element_type=jnp.float32)
    grad_value = jnp.einsum("htk,thd->kd", weights_low, block_g, preferred_element_type=jnp.float32)
    return (output, grad_query, grad_key, grad_value)


def body(queries, key_vectors, value_vectors, output_gradient, doc_lengths):
    ctx_index = lax.axis_index("ctx")
    k_heads, v_heads = (
        lax.all_to_all(key_vectors, "tp", split_axis=1, concat_axis=0, tiled=True),
        lax.all_to_all(value_vectors, "tp", split_axis=1, concat_axis=0, tiled=True),
    )
    shard_len = queries.shape[0]
    kv_groups = k_heads.shape[1] // HEAD_SIZE
    row_goal = max(1, 512 // shard_len)
    score_scale = 1.0 / math.sqrt(HEAD_SIZE)
    kv_local = jnp.concatenate([k_heads, v_heads], axis=1)
    feature_count = kv_local.shape[1]
    slot_list = [kv_local]
    for offset in range(1, WINDOW):
        slot_list.append(shifted(kv_local, "ctx", offset))
    window = jnp.stack(slot_list, axis=0)
    doc_starts = jnp.cumsum(doc_lengths, dtype=jnp.int32) - doc_lengths
    local_pos = jnp.arange(shard_len, dtype=jnp.int32)
    slot_index = jnp.arange(WINDOW, dtype=jnp.int32)
    first_pos = ctx_index * shard_len
    query_pos = first_pos + local_pos
    query_doc = doc_index_of(query_pos, doc_starts)
    key_pos = ((ctx_index - slot_index)[:, None] * shard_len + local_pos[None, :]).reshape(-1)
    key_doc = doc_index_of(key_pos, doc_starts)
    doc_start = jnp.max(jnp.where(doc_starts <= first_pos, doc_starts, 0))
    needed = jnp.clip(ctx_index - doc_start // shard_len + 1, 1, WINDOW)
    query_pos, query_doc, key_pos, key_doc, needed = (
        query_pos,
        query_doc,
        key_pos,
        key_doc,
        needed,
    )
    local_heads = queries.shape[1] // HEAD_SIZE // kv_groups
    head_block = max(
        [
            candidate
            for candidate in range(1, local_heads + 1)
            if local_heads % candidate == 0 and candidate <= row_goal
        ]
    )
    per_group = local_heads // head_block
    block_total = kv_groups * per_group
    key_total_count = WINDOW * shard_len
    allowed = (query_doc[:, None] == key_doc[None, :key_total_count]) & (
        key_pos[None, :key_total_count] <= query_pos[:, None]
    )
    flat_window = window.reshape(key_total_count, feature_count)

    def one_block(number, buffers):
        out_buf, grad_q_buf, grad_window = buffers
        group_index = number // per_group
        column = (group_index * local_heads + number % per_group * head_block) * HEAD_SIZE
        block_q = lax.dynamic_slice_in_dim(queries, column, head_block * HEAD_SIZE, 1).reshape(
            shard_len, head_block, HEAD_SIZE
        )
        block_g = lax.dynamic_slice_in_dim(
            output_gradient, column, head_block * HEAD_SIZE, 1
        ).reshape(shard_len, head_block, HEAD_SIZE)
        key_col = group_index * HEAD_SIZE
        value_col = (kv_groups + group_index) * HEAD_SIZE
        key_block = lax.dynamic_slice_in_dim(flat_window, key_col, HEAD_SIZE, 1)
        value_block = lax.dynamic_slice_in_dim(flat_window, value_col, HEAD_SIZE, 1)
        output, grad_query, grad_key, grad_value = attend_block(
            block_q, block_g, key_block, value_block, allowed, score_scale
        )
        out_buf = lax.dynamic_update_slice_in_dim(
            out_buf, output.reshape(shard_len, head_block * HEAD_SIZE), column, 1
        )
        grad_q_buf = lax.dynamic_update_slice_in_dim(
            grad_q_buf, grad_query.reshape(shard_len, head_block * HEAD_SIZE), column, 1
        )
        grad_window = lax.dynamic_update_slice_in_dim(
            grad_window,
            lax.dynamic_slice_in_dim(grad_window, key_col, HEAD_SIZE, 1) + grad_key,
            key_col,
            1,
        )
        grad_window = lax.dynamic_update_slice_in_dim(
            grad_window,
            lax.dynamic_slice_in_dim(grad_window, value_col, HEAD_SIZE, 1) + grad_value,
            value_col,
            1,
        )
        return (out_buf, grad_q_buf, grad_window)

    initial_state = (
        jnp.zeros_like(queries),
        jnp.zeros_like(queries),
        jnp.zeros((key_total_count, feature_count), jnp.float32),
    )
    out_buf, grad_q_buf, grad_window = lax.fori_loop(0, block_total, one_block, initial_state)
    grad_window = grad_window.reshape(WINDOW, shard_len, feature_count)
    out_heads, dq_heads, grad_window = (out_buf, grad_q_buf, grad_window)
    grad_own = grad_window[0]
    for offset in range(1, WINDOW):
        grad_own = grad_own + shifted(
            grad_window[offset].astype(jnp.bfloat16), "ctx", -offset
        ).astype(jnp.float32)
    grad_k_heads = grad_own[:, : kv_groups * HEAD_SIZE].astype(jnp.bfloat16)
    grad_v_heads = grad_own[:, kv_groups * HEAD_SIZE :].astype(jnp.bfloat16)
    key_gradient, value_gradient = (
        lax.all_to_all(grad_k_heads, "tp", split_axis=0, concat_axis=1, tiled=True),
        lax.all_to_all(grad_v_heads, "tp", split_axis=0, concat_axis=1, tiled=True),
    )
    return (out_heads, dq_heads, key_gradient, value_gradient)


def solution(mesh):
    return jax.shard_map(
        body,
        mesh=mesh,
        in_specs=(
            P("ctx", "tp"),
            P(("ctx", "tp"), None),
            P(("ctx", "tp"), None),
            P("ctx", "tp"),
            P(),
        ),
        out_specs=(P("ctx", "tp"), P("ctx", "tp"), P(("ctx", "tp"), None), P(("ctx", "tp"), None)),
        check_vma=False,
    )
```

profile of v0, /device:TPU:6, one launch (start us, length us, event | category | flops | bytes accessed | tf_op | source)
XLA Modules:
  0.0 214.0 jit_solution(13816212506503750472)
XLA Ops:
  2.1 7.1 %all-to-all-start.1 = ((bf16[32,8,128]{2,0,1:T(8,128)(2,1)}), bf16[32,8,128]{2,0,1:T(8,128)(2,1)S(1)}, u32[]{:S(2)}, u32[]{:S(2)}) async-start(bf16[32,8,128]{2,0,1:T(8,128)(2,1)} %copy_bitcast_fusion.2), calls=%async_computation.1 | async-start | bytes 131072 | tf_op jit(solution)/shard_map/all_to_all | solution.py:55
  9.2 1.5 copy_bitcast_fusion.3
  12.5 5.1 %all-to-all-done.1 = bf16[32,8,128]{2,0,1:T(8,128)(2,1)S(1)} async-done(((bf16[32,8,128]{2,0,1:T(8,128)(2,1)}), bf16[32,8,128]{2,0,1:T(8,128)(2,1)S(1)}, u32[]{:S(2)}, u32[]{:S(2)}) %all-to-all-start.1) | async-done | bytes 65568 | tf_op jit(solution)/shard_map/all_to_all | solution.py:55
  17.6 3.4 %all-to-all-start = ((bf16[32,8,128]{2,0,1:T(8,128)(2,1)}), bf16[32,8,128]{2,0,1:T(8,128)(2,1)S(1)}, u32[]{:S(2)}, u32[]{:S(2)}) async-start(bf16[32,8,128]{2,0,1:T(8,128)(2,1)} %copy_bitcast_fusion.3), calls=%async_computation | async-start | bytes 131072 | tf_op jit(solution)/shard_map/all_to_all | solution.py:54
  21.1 8.2 %all-to-all-done = bf16[32,8,128]{2,0,1:T(8,128)(2,1)S(1)} async-done(((bf16[32,8,128]{2,0,1:T(8,128)(2,1)}), bf16[32,8,128]{2,0,1:T(8,128)(2,1)S(1)}, u32[]{:S(2)}, u32[]{:S(2)}) %all-to-all-start) | async-done | bytes 65568 | tf_op jit(solution)/shard_map/all_to_all | solution.py:54
  29.3 1.9 collective-permute-start
  31.2 4.2 %collective-permute-start.1 = (bf16[256,256]{1,0:T(8,128)(2,1)S(1)}, bf16[256,256]{1,0:T(8,128)(2,1)S(1)}, u32[]{:S(2)}, u32[]{:S(2)}) collective-permute-start(bf16[256,256]{1,0:T(8,128)(2,1)S(1)} %pad_maximum_fusion), channel_id=1, source_target_pairs={{0,16},{8,24},{16,32},{24,40},{32,48},{40,56},{48,64},{56,72},{64,... | collective-permute-start | bytes 393224 | tf_op jit(solution)/shard_map/ppermute | solution.py:15
  35.4 4.3 %collective-permute-start.2 = (bf16[256,256]{1,0:T(8,128)(2,1)S(1)}, bf16[256,256]{1,0:T(8,128)(2,1)S(1)}, u32[]{:S(2)}, u32[]{:S(2)}) collective-permute-start(bf16[256,256]{1,0:T(8,128)(2,1)S(1)} %pad_maximum_fusion), channel_id=1, source_target_pairs={{0,24},{8,32},{16,40},{24,48},{32,56},{40,64},{48,72},{56,80},{64,... | collective-permute-start | bytes 393224 | tf_op jit(solution)/shard_map/ppermute | solution.py:15
  39.7 4.8 %collective-permute-start.3 = (bf16[256,256]{1,0:T(8,128)(2,1)S(1)}, bf16[256,256]{1,0:T(8,128)(2,1)S(1)}, u32[]{:S(2)}, u32[]{:S(2)}) collective-permute-start(bf16[256,256]{1,0:T(8,128)(2,1)S(1)} %pad_maximum_fusion), channel_id=1, source_target_pairs={{0,32},{8,40},{16,48},{24,56},{32,64},{40,72},{48,80},{56,88},{64,... | collective-permute-start | bytes 393224 | tf_op jit(solution)/shard_map/ppermute | solution.py:15
  44.6 3.8 %collective-permute-start.4 = (bf16[256,256]{1,0:T(8,128)(2,1)S(1)}, bf16[256,256]{1,0:T(8,128)(2,1)S(1)}, u32[]{:S(2)}, u32[]{:S(2)}) collective-permute-start(bf16[256,256]{1,0:T(8,128)(2,1)S(1)} %pad_maximum_fusion), channel_id=1, source_target_pairs={{0,40},{8,48},{16,56},{24,64},{32,72},{40,80},{48,88},{56,96},{64,... | collective-permute-start | bytes 393224 | tf_op jit(solution)/shard_map/ppermute | solution.py:15
  48.4 3.6 %collective-permute-start.5 = (bf16[256,256]{1,0:T(8,128)(2,1)S(1)}, bf16[256,256]{1,0:T(8,128)(2,1)S(1)}, u32[]{:S(2)}, u32[]{:S(2)}) collective-permute-start(bf16[256,256]{1,0:T(8,128)(2,1)S(1)} %pad_maximum_fusion), channel_id=1, source_target_pairs={{0,48},{8,56},{16,64},{24,72},{32,80},{40,88},{48,96},{56,104},{64... | collective-permute-start | bytes 393224 | tf_op jit(solution)/shard_map/ppermute | solution.py:15
  52.1 6.1 %collective-permute-start.6 = (bf16[256,256]{1,0:T(8,128)(2,1)S(1)}, bf16[256,256]{1,0:T(8,128)(2,1)S(1)}, u32[]{:S(2)}, u32[]{:S(2)}) collective-permute-start(bf16[256,256]{1,0:T(8,128)(2,1)S(1)} %pad_maximum_fusion), channel_id=1, source_target_pairs={{0,56},{8,64},{16,72},{24,80},{32,88},{40,96},{48,104},{56,112},{6... | collective-permute-start | bytes 393224 | tf_op jit(solution)/shard_map/ppermute | solution.py:15
  58.3 2.6 %collective-permute-done.6 = bf16[256,256]{1,0:T(8,128)(2,1)S(1)} collective-permute-done((bf16[256,256]{1,0:T(8,128)(2,1)S(1)}, bf16[256,256]{1,0:T(8,128)(2,1)S(1)}, u32[]{:S(2)}, u32[]{:S(2)}) %collective-permute-start.6) | collective-permute-done | bytes 131104 | tf_op jit(solution)/shard_map/ppermute | solution.py:15
  62.6 1.5 broadcast_in_dim.53
  64.1 98.8 %while.20 = (s32[]{:T(128)}, bf16[256,1024]{1,0:T(8,128)(2,1)}, bf16[256,1024]{1,0:T(8,128)(2,1)}, f32[2048,256]{1,0:T(8,128)}, bf16[2048,256]{1,0:T(8,128)(2,1)...) while((s32[]{:T(128)}, bf16[256,1024]{1,0:T(8,128)(2,1)}, ...), condition=%wide.region_7.8_spmd.clone, body=%wide.region_3.7_spmd.clone.sunk | while | flops 1627782144 | bytes 81699448 | solution.py:142
  65.2 1.4 compare_and_fusion.2
  66.7 2.7 %fusion.59 = (f32[2,256]{1,0:T(2,128)S(1)}, f32[2,256,2048]{1,2,0:T(8,128)}) fusion(bf16[256,2,128]{0,2,1:T(8,128)(2,1)S(1)} %bitcast.149, bf16[2048,256]{1,0:T(8,128)(2,1)S(1)} %get-tuple-element.475, s32[]{:T(128)S(6)} %select_n.95, pred[256,2048]{0,1:T(8,128)(4,1)S(1)} %compare_and_fusion.2), kind=kOutput, calls=%fused_computation.57.clone.1 | convolution fusion | flops 271580672 | bytes 5376004 | tf_op jit(solution)/shard_map/while/body/eval_jaxpr/thd,kd->htk/dot_general | solution.py:25
  70.4 2.8 %exponential_reduce_fusion.2 = f32[2,256]{1,0:T(2,128)S(1)} fusion(f32[2,256,2048]{1,2,0:T(8,128)} %get-tuple-element.423, f32[2,256]{1,0:T(2,128)S(1)} %get-tuple-element.424), kind=kLoop, calls=%fused_computation.7.clone.1 | loop fusion | flops 2096640 | bytes 4198400 | tf_op jit(solution)/shard_map/while/body/eval_jaxpr/reduce_sum | solution.py:30
  73.8 3.8 %multiply_reduce_fusion.2 = (f32[256,2]{0,1:T(2,128)S(1)}, bf16[128,2,256]{2,0,1:T(8,128)(2,1)}) fusion(bf16[256,256]{0,1:T(8,128)(2,1)S(1)} %copy.123, f32[2,256,2048]{1,2,0:T(8,128)} %get-tuple-element.423, f32[2,256]{1,0:T(2,128)S(1)} %log_add_fusion.2, bf16[2048,256]{0,1:T(8,128)(2,1)S(1)} %copy.124, s32[]{:T(128)S(6)} %select_n.96), kind=kOutput, calls=%fused_computation.26.clone.1 | convolution fusion | flops 270859776 | bytes 4984836 | tf_op jit(solution)/shard_map/while/body/eval_jaxpr/htk,kd->thd/dot_general | solution.py:34
  77.6 1.3 fusion.60
  78.9 1.5 convolution_convert_fusion.3
  82.3 3.4 %fusion.61 = f32[2048,256]{1,0:T(8,128)} fusion(f32[2048,256]{1,0:T(8,128)} %get-tuple-element.453, s32[]{:T(128)S(6)} %select_n.95, bf16[2,256,2048]{1,2,0:T(8,128)(2,1)S(1)} %fusion.60, bf16[256,2,128]{0,2,1:T(8,128)(2,1)S(1)} %bitcast.150), kind=kOutput, calls=%fused_computation.12.clone.1 | convolution fusion | flops 268697600 | bytes 4325380 | tf_op jit(solution)/shard_map/while/body/eval_jaxpr/htk,thd->kd/dot_general | solution.py:46
  85.7 3.1 %fusion.62 = f32[2048,256]{1,0:T(8,128)} fusion(f32[2048,256]{1,0:T(8,128)} %fusion.61, s32[]{:T(128)S(6)} %select_n.96, bf16[256,2,128]{0,2,1:T(8,128)(2,1)S(1)} %bitcast.148, f32[2,256,2048]{1,2,0:T(8,128)S(1)} %copy-done.2, f32[2,256]{1,0:T(2,128)S(1)} %log_add_fusion.2), kind=kOutput, calls=%fused_computation.14.clone.1 | convolution fusion | flops 270794752 | bytes 6424580 | tf_op jit(solution)/shard_map/while/body/eval_jaxpr/htk,thd->kd/dot_general | solution.py:47
  88.8 1.0 constant_dynamic-slice_fusion.4
  89.9 1.4 compare_and_fusion.2
  91.4 2.7 %fusion.59 = (f32[2,256]{1,0:T(2,128)S(1)}, f32[2,256,2048]{1,2,0:T(8,128)}) fusion(bf16[256,2,128]{0,2,1:T(8,128)(2,1)S(1)} %bitcast.149, bf16[2048,256]{1,0:T(8,128)(2,1)S(1)} %get-tuple-element.475, s32[]{:T(128)S(6)} %select_n.95, pred[256,2048]{0,1:T(8,128)(4,1)S(1)} %compare_and_fusion.2), kind=kOutput, calls=%fused_computation.57.clone.1 | convolution fusion | flops 271580672 | bytes 5376004 | tf_op jit(solution)/shard_map/while/body/eval_jaxpr/thd,kd->htk/dot_general | solution.py:25
  95.1 2.8 %exponential_reduce_fusion.2 = f32[2,256]{1,0:T(2,128)S(1)} fusion(f32[2,256,2048]{1,2,0:T(8,128)} %get-tuple-element.423, f32[2,256]{1,0:T(2,128)S(1)} %get-tuple-element.424), kind=kLoop, calls=%fused_computation.7.clone.1 | loop fusion | flops 2096640 | bytes 4198400 | tf_op jit(solution)/shard_map/while/body/eval_jaxpr/reduce_sum | solution.py:30
  98.5 3.8 %multiply_reduce_fusion.2 = (f32[256,2]{0,1:T(2,128)S(1)}, bf16[128,2,256]{2,0,1:T(8,128)(2,1)}) fusion(bf16[256,256]{0,1:T(8,128)(2,1)S(1)} %copy.123, f32[2,256,2048]{1,2,0:T(8,128)} %get-tuple-element.423, f32[2,256]{1,0:T(2,128)S(1)} %log_add_fusion.2, bf16[2048,256]{0,1:T(8,128)(2,1)S(1)} %copy.124, s32[]{:T(128)S(6)} %select_n.96), kind=kOutput, calls=%fused_computation.26.clone.1 | convolution fusion | flops 270859776 | bytes 4984836 | tf_op jit(solution)/shard_map/while/body/eval_jaxpr/htk,kd->thd/dot_general | solution.py:34
  102.4 1.3 fusion.60
  103.6 1.5 convolution_convert_fusion.3
  107.0 3.4 %fusion.61 = f32[2048,256]{1,0:T(8,128)} fusion(f32[2048,256]{1,0:T(8,128)} %get-tuple-element.453, s32[]{:T(128)S(6)} %select_n.95, bf16[2,256,2048]{1,2,0:T(8,128)(2,1)S(1)} %fusion.60, bf16[256,2,128]{0,2,1:T(8,128)(2,1)S(1)} %bitcast.150), kind=kOutput, calls=%fused_computation.12.clone.1 | convolution fusion | flops 268697600 | bytes 4325380 | tf_op jit(solution)/shard_map/while/body/eval_jaxpr/htk,thd->kd/dot_general | solution.py:46
  110.4 3.1 %fusion.62 = f32[2048,256]{1,0:T(8,128)} fusion(f32[2048,256]{1,0:T(8,128)} %fusion.61, s32[]{:T(128)S(6)} %select_n.96, bf16[256,2,128]{0,2,1:T(8,128)(2,1)S(1)} %bitcast.148, f32[2,256,2048]{1,2,0:T(8,128)S(1)} %copy-done.2, f32[2,256]{1,0:T(2,128)S(1)} %log_add_fusion.2), kind=kOutput, calls=%fused_computation.14.clone.1 | convolution fusion | flops 270794752 | bytes 6424580 | tf_op jit(solution)/shard_map/while/body/eval_jaxpr/htk,thd->kd/dot_general | solution.py:47
  113.5 1.0 constant_dynamic-slice_fusion.4
  114.6 1.4 compare_and_fusion.2
  116.1 2.7 %fusion.59 = (f32[2,256]{1,0:T(2,128)S(1)}, f32[2,256,2048]{1,2,0:T(8,128)}) fusion(bf16[256,2,128]{0,2,1:T(8,128)(2,1)S(1)} %bitcast.149, bf16[2048,256]{1,0:T(8,128)(2,1)S(1)} %get-tuple-element.475, s32[]{:T(128)S(6)} %select_n.95, pred[256,2048]{0,1:T(8,128)(4,1)S(1)} %compare_and_fusion.2), kind=kOutput, calls=%fused_computation.57.clone.1 | convolution fusion | flops 271580672 | bytes 5376004 | tf_op jit(solution)/shard_map/while/body/eval_jaxpr/thd,kd->htk/dot_general | solution.py:25
  119.8 2.8 %exponential_reduce_fusion.2 = f32[2,256]{1,0:T(2,128)S(1)} fusion(f32[2,256,2048]{1,2,0:T(8,128)} %get-tuple-element.423, f32[2,256]{1,0:T(2,128)S(1)} %get-tuple-element.424), kind=kLoop, calls=%fused_computation.7.clone.1 | loop fusion | flops 2096640 | bytes 4198400 | tf_op jit(solution)/shard_map/while/body/eval_jaxpr/reduce_sum | solution.py:30
  123.2 3.8 %multiply_reduce_fusion.2 = (f32[256,2]{0,1:T(2,128)S(1)}, bf16[128,2,256]{2,0,1:T(8,128)(2,1)}) fusion(bf16[256,256]{0,1:T(8,128)(2,1)S(1)} %copy.123, f32[2,256,2048]{1,2,0:T(8,128)} %get-tuple-element.423, f32[2,256]{1,0:T(2,128)S(1)} %log_add_fusion.2, bf16[2048,256]{0,1:T(8,128)(2,1)S(1)} %copy.124, s32[]{:T(128)S(6)} %select_n.96), kind=kOutput, calls=%fused_computation.26.clone.1 | convolution fusion | flops 270859776 | bytes 4984836 | tf_op jit(solution)/shard_map/while/body/eval_jaxpr/htk,kd->thd/dot_general | solution.py:34
  127.1 1.3 fusion.60
  128.3 1.5 convolution_convert_fusion.3
  131.7 3.4 %fusion.61 = f32[2048,256]{1,0:T(8,128)} fusion(f32[2048,256]{1,0:T(8,128)} %get-tuple-element.453, s32[]{:T(128)S(6)} %select_n.95, bf16[2,256,2048]{1,2,0:T(8,128)(2,1)S(1)} %fusion.60, bf16[256,2,128]{0,2,1:T(8,128)(2,1)S(1)} %bitcast.150), kind=kOutput, calls=%fused_computation.12.clone.1 | convolution fusion | flops 268697600 | bytes 4325380 | tf_op jit(solution)/shard_map/while/body/eval_jaxpr/htk,thd->kd/dot_general | solution.py:46
  135.1 3.1 %fusion.62 = f32[2048,256]{1,0:T(8,128)} fusion(f32[2048,256]{1,0:T(8,128)} %fusion.61, s32[]{:T(128)S(6)} %select_n.96, bf16[256,2,128]{0,2,1:T(8,128)(2,1)S(1)} %bitcast.148, f32[2,256,2048]{1,2,0:T(8,128)S(1)} %copy-done.2, f32[2,256]{1,0:T(2,128)S(1)} %log_add_fusion.2), kind=kOutput, calls=%fused_computation.14.clone.1 | convolution fusion | flops 270794752 | bytes 6424580 | tf_op jit(solution)/shard_map/while/body/eval_jaxpr/htk,thd->kd/dot_general | solution.py:47
  139.3 1.4 compare_and_fusion.2
  140.8 2.7 %fusion.59 = (f32[2,256]{1,0:T(2,128)S(1)}, f32[2,256,2048]{1,2,0:T(8,128)}) fusion(bf16[256,2,128]{0,2,1:T(8,128)(2,1)S(1)} %bitcast.149, bf16[2048,256]{1,0:T(8,128)(2,1)S(1)} %get-tuple-element.475, s32[]{:T(128)S(6)} %select_n.95, pred[256,2048]{0,1:T(8,128)(4,1)S(1)} %compare_and_fusion.2), kind=kOutput, calls=%fused_computation.57.clone.1 | convolution fusion | flops 271580672 | bytes 5376004 | tf_op jit(solution)/shard_map/while/body/eval_jaxpr/thd,kd->htk/dot_general | solution.py:25
  144.5 2.8 %exponential_reduce_fusion.2 = f32[2,256]{1,0:T(2,128)S(1)} fusion(f32[2,256,2048]{1,2,0:T(8,128)} %get-tuple-element.423, f32[2,256]{1,0:T(2,128)S(1)} %get-tuple-element.424), kind=kLoop, calls=%fused_computation.7.clone.1 | loop fusion | flops 2096640 | bytes 4198400 | tf_op jit(solution)/shard_map/while/body/eval_jaxpr/reduce_sum | solution.py:30
  147.9 3.8 %multiply_reduce_fusion.2 = (f32[256,2]{0,1:T(2,128)S(1)}, bf16[128,2,256]{2,0,1:T(8,128)(2,1)}) fusion(bf16[256,256]{0,1:T(8,128)(2,1)S(1)} %copy.123, f32[2,256,2048]{1,2,0:T(8,128)} %get-tuple-element.423, f32[2,256]{1,0:T(2,128)S(1)} %log_add_fusion.2, bf16[2048,256]{0,1:T(8,128)(2,1)S(1)} %copy.124, s32[]{:T(128)S(6)} %select_n.96), kind=kOutput, calls=%fused_computation.26.clone.1 | convolution fusion | flops 270859776 | bytes 4984836 | tf_op jit(solution)/shard_map/while/body/eval_jaxpr/htk,kd->thd/dot_general | solution.py:34
  151.8 1.3 fusion.60
  153.0 1.5 convolution_convert_fusion.3
  156.4 3.4 %fusion.61 = f32[2048,256]{1,0:T(8,128)} fusion(f32[2048,256]{1,0:T(8,128)} %get-tuple-element.453, s32[]{:T(128)S(6)} %select_n.95, bf16[2,256,2048]{1,2,0:T(8,128)(2,1)S(1)} %fusion.60, bf16[256,2,128]{0,2,1:T(8,128)(2,1)S(1)} %bitcast.150), kind=kOutput, calls=%fused_computation.12.clone.1 | convolution fusion | flops 268697600 | bytes 4325380 | tf_op jit(solution)/shard_map/while/body/eval_jaxpr/htk,thd->kd/dot_general | solution.py:46
  159.8 3.1 %fusion.62 = f32[2048,256]{1,0:T(8,128)} fusion(f32[2048,256]{1,0:T(8,128)} %fusion.61, s32[]{:T(128)S(6)} %select_n.96, bf16[256,2,128]{0,2,1:T(8,128)(2,1)S(1)} %bitcast.148, f32[2,256,2048]{1,2,0:T(8,128)S(1)} %copy-done.2, f32[2,256]{1,0:T(2,128)S(1)} %log_add_fusion.2), kind=kOutput, calls=%fused_computation.14.clone.1 | convolution fusion | flops 270794752 | bytes 6424580 | tf_op jit(solution)/shard_map/while/body/eval_jaxpr/htk,thd->kd/dot_general | solution.py:47
  162.9 1.7 convert.13
  164.6 1.3 collective-permute-start.13
  165.9 1.9 collective-permute-start.12
  167.9 1.9 collective-permute-start.11
  169.8 1.9 collective-permute-start.10
  171.7 1.9 collective-permute-start.9
  173.7 2.8 %collective-permute-start.8 = (bf16[256,256]{1,0:T(8,128)(2,1)S(1)}, bf16[256,256]{1,0:T(8,128)(2,1)S(1)}, u32[]{:S(2)}, u32[]{:S(2)}) collective-permute-start(bf16[256,256]{1,0:T(8,128)(2,1)S(1)} %get-tuple-element.347), channel_id=1, source_target_pairs={{16,0},{24,8},{32,16},{40,24},{48,32},{56,40},{64,48},{72,56},{80,... | collective-permute-start | bytes 393224 | tf_op jit(solution)/shard_map/ppermute | solution.py:15
  176.5 3.2 %collective-permute-start.7 = (bf16[256,256]{1,0:T(8,128)(2,1)S(1)}, bf16[256,256]{1,0:T(8,128)(2,1)S(1)}, u32[]{:S(2)}, u32[]{:S(2)}) collective-permute-start(bf16[256,256]{1,0:T(8,128)(2,1)S(1)} %get-tuple-element.341), channel_id=1, source_target_pairs={{8,0},{16,8},{24,16},{32,24},{40,32},{48,40},{56,48},{64,56},{72,6... | collective-permute-start | bytes 393224 | tf_op jit(solution)/shard_map/ppermute | solution.py:15
  180.6 2.6 %collective-permute-done.10 = bf16[256,256]{1,0:T(8,128)(2,1)S(1)} collective-permute-done((bf16[256,256]{1,0:T(8,128)(2,1)S(1)}, bf16[256,256]{1,0:T(8,128)(2,1)S(1)}, u32[]{:S(2)}, u32[]{:S(2)}) %collective-permute-start.10) | collective-permute-done | bytes 131104 | tf_op jit(solution)/shard_map/ppermute | solution.py:15
  183.2 1.7 collective-permute-done.9
  185.0 3.6 %collective-permute-done.8 = bf16[256,256]{1,0:T(8,128)(2,1)S(1)} collective-permute-done((bf16[256,256]{1,0:T(8,128)(2,1)S(1)}, bf16[256,256]{1,0:T(8,128)(2,1)S(1)}, u32[]{:S(2)}, u32[]{:S(2)}) %collective-permute-start.8) | collective-permute-done | bytes 131104 | tf_op jit(solution)/shard_map/ppermute | solution.py:15
  188.6 1.1 add_convert_fusion
  190.3 11.3 %all_to_all.76 = bf16[8,32,128]{2,1,0:T(8,128)(2,1)S(1)} all-to-all(bf16[8,32,128]{2,1,0:T(8,128)(2,1)S(1)} %bitcast.159), channel_id=1, replica_groups=mesh['ctx'=64,'tp'=8] {'tp'}, dimensions={0} | all-to-all | bytes 131072 | tf_op jit(solution)/shard_map/all_to_all | solution.py:153
  201.7 3.4 %all-to-all-start.3 = ((bf16[8,32,128]{2,1,0:T(8,128)(2,1)}), bf16[8,32,128]{2,1,0:T(8,128)(2,1)S(1)}, u32[]{:S(2)}, u32[]{:S(2)}) async-start(bf16[8,32,128]{2,1,0:T(8,128)(2,1)} %bitcast.16), calls=%async_computation.3 | async-start | bytes 131072 | tf_op jit(solution)/shard_map/all_to_all | solution.py:154
  205.7 7.7 %all-to-all-done.3 = bf16[8,32,128]{2,1,0:T(8,128)(2,1)S(1)} async-done(((bf16[8,32,128]{2,1,0:T(8,128)(2,1)}), bf16[8,32,128]{2,1,0:T(8,128)(2,1)S(1)}, u32[]{:S(2)}, u32[]{:S(2)}) %all-to-all-start.3) | async-done | bytes 65568 | tf_op jit(solution)/shard_map/all_to_all | solution.py:154
  (106 shorter events, 24.6 us)
Async XLA Ops:
  0.6 0.8 copy-start
  2.1 15.5 %all-to-all-start.1 = ((bf16[32,8,128]{2,0,1:T(8,128)(2,1)}), bf16[32,8,128]{2,0,1:T(8,128)(2,1)S(1)}, u32[]{:S(2)}, u32[]{:S(2)}) async-start(bf16[32,8,128]{2,0,1:T(8,128)(2,1)} %copy_bitcast_fusion.2), calls=%async_computation.1 | async-start | bytes 131072 | tf_op jit(solution)/shard_map/all_to_all | solution.py:55
  17.6 11.7 %all-to-all-start = ((bf16[32,8,128]{2,0,1:T(8,128)(2,1)}), bf16[32,8,128]{2,0,1:T(8,128)(2,1)S(1)}, u32[]{:S(2)}, u32[]{:S(2)}) async-start(bf16[32,8,128]{2,0,1:T(8,128)(2,1)} %copy_bitcast_fusion.3), calls=%async_computation | async-start | bytes 131072 | tf_op jit(solution)/shard_map/all_to_all | solution.py:54
  29.3 19.1 %collective-permute-start = (bf16[256,256]{1,0:T(8,128)(2,1)S(1)}, bf16[256,256]{1,0:T(8,128)(2,1)S(1)}, u32[]{:S(2)}, u32[]{:S(2)}) collective-permute-start(bf16[256,256]{1,0:T(8,128)(2,1)S(1)} %pad_maximum_fusion), channel_id=1, source_target_pairs={{0,8},{8,16},{16,24},{24,32},{32,40},{40,48},{48,56},{56,64},{64,7... | collective-permute-start | bytes 393224 | tf_op jit(solution)/shard_map/ppermute | solution.py:15
  31.2 20.9 %collective-permute-start.1 = (bf16[256,256]{1,0:T(8,128)(2,1)S(1)}, bf16[256,256]{1,0:T(8,128)(2,1)S(1)}, u32[]{:S(2)}, u32[]{:S(2)}) collective-permute-start(bf16[256,256]{1,0:T(8,128)(2,1)S(1)} %pad_maximum_fusion), channel_id=1, source_target_pairs={{0,16},{8,24},{16,32},{24,40},{32,48},{40,56},{48,64},{56,72},{64,... | collective-permute-start | bytes 393224 | tf_op jit(solution)/shard_map/ppermute | solution.py:15
  35.4 22.8 %collective-permute-start.2 = (bf16[256,256]{1,0:T(8,128)(2,1)S(1)}, bf16[256,256]{1,0:T(8,128)(2,1)S(1)}, u32[]{:S(2)}, u32[]{:S(2)}) collective-permute-start(bf16[256,256]{1,0:T(8,128)(2,1)S(1)} %pad_maximum_fusion), channel_id=1, source_target_pairs={{0,24},{8,32},{16,40},{24,48},{32,56},{40,64},{48,72},{56,80},{64,... | collective-permute-start | bytes 393224 | tf_op jit(solution)/shard_map/ppermute | solution.py:15
  39.7 18.5 %collective-permute-start.3 = (bf16[256,256]{1,0:T(8,128)(2,1)S(1)}, bf16[256,256]{1,0:T(8,128)(2,1)S(1)}, u32[]{:S(2)}, u32[]{:S(2)}) collective-permute-start(bf16[256,256]{1,0:T(8,128)(2,1)S(1)} %pad_maximum_fusion), channel_id=1, source_target_pairs={{0,32},{8,40},{16,48},{24,56},{32,64},{40,72},{48,80},{56,88},{64,... | collective-permute-start | bytes 393224 | tf_op jit(solution)/shard_map/ppermute | solution.py:15
  44.6 13.7 %collective-permute-start.4 = (bf16[256,256]{1,0:T(8,128)(2,1)S(1)}, bf16[256,256]{1,0:T(8,128)(2,1)S(1)}, u32[]{:S(2)}, u32[]{:S(2)}) collective-permute-start(bf16[256,256]{1,0:T(8,128)(2,1)S(1)} %pad_maximum_fusion), channel_id=1, source_target_pairs={{0,40},{8,48},{16,56},{24,64},{32,72},{40,80},{48,88},{56,96},{64,... | collective-permute-start | bytes 393224 | tf_op jit(solution)/shard_map/ppermute | solution.py:15
  48.4 9.9 %collective-permute-start.5 = (bf16[256,256]{1,0:T(8,128)(2,1)S(1)}, bf16[256,256]{1,0:T(8,128)(2,1)S(1)}, u32[]{:S(2)}, u32[]{:S(2)}) collective-permute-start(bf16[256,256]{1,0:T(8,128)(2,1)S(1)} %pad_maximum_fusion), channel_id=1, source_target_pairs={{0,48},{8,56},{16,64},{24,72},{32,80},{40,88},{48,96},{56,104},{64... | collective-permute-start | bytes 393224 | tf_op jit(solution)/shard_map/ppermute | solution.py:15
  52.1 8.8 %collective-permute-start.6 = (bf16[256,256]{1,0:T(8,128)(2,1)S(1)}, bf16[256,256]{1,0:T(8,128)(2,1)S(1)}, u32[]{:S(2)}, u32[]{:S(2)}) collective-permute-start(bf16[256,256]{1,0:T(8,128)(2,1)S(1)} %pad_maximum_fusion), channel_id=1, source_target_pairs={{0,56},{8,64},{16,72},{24,80},{32,88},{40,96},{48,104},{56,112},{6... | collective-permute-start | bytes 393224 | tf_op jit(solution)/shard_map/ppermute | solution.py:15
  64.1 9.1 %copy-start.3 = (bf16[2048,256]{1,0:T(8,128)(2,1)}, bf16[2048,256]{1,0:T(8,128)(2,1)S(1)}, u32[]{:S(2)}) copy-start(bf16[2048,256]{1,0:T(8,128)(2,1)S(1)} %get-tuple-element.475) | copy-start | bytes 3145732 | tf_op jit(solution)/shard_map/while
  73.8 3.9 %copy-start.1 = (f32[2,256,2048]{1,2,0:T(8,128)S(1)}, f32[2,256,2048]{1,2,0:T(8,128)}, u32[]{:S(2)}) copy-start(f32[2,256,2048]{1,2,0:T(8,128)} %get-tuple-element.423) | copy-start | bytes 12582916 | tf_op jit(solution)/shard_map/while
  81.6 4.1 %copy-start.2 = (f32[2,256,2048]{1,2,0:T(8,128)S(1)}, f32[2,256,2048]{1,2,0:T(8,128)}, u32[]{:S(2)}) copy-start(f32[2,256,2048]{1,2,0:T(8,128)} %get-tuple-element.423) | copy-start | bytes 12582916 | tf_op jit(solution)/shard_map/while
  85.7 3.1 %copy-start.4 = (bf16[2048,256]{1,0:T(8,128)(2,1)S(1)}, bf16[2048,256]{1,0:T(8,128)(2,1)}, u32[]{:S(2)}) copy-start(bf16[2048,256]{1,0:T(8,128)(2,1)} %copy-done.3) | copy-start | bytes 3145732 | tf_op jit(solution)/shard_map/while
  88.8 9.1 %copy-start.3 = (bf16[2048,256]{1,0:T(8,128)(2,1)}, bf16[2048,256]{1,0:T(8,128)(2,1)S(1)}, u32[]{:S(2)}) copy-start(bf16[2048,256]{1,0:T(8,128)(2,1)S(1)} %get-tuple-element.475) | copy-start | bytes 3145732 | tf_op jit(solution)/shard_map/while
  98.5 3.9 %copy-start.1 = (f32[2,256,2048]{1,2,0:T(8,128)S(1)}, f32[2,256,2048]{1,2,0:T(8,128)}, u32[]{:S(2)}) copy-start(f32[2,256,2048]{1,2,0:T(8,128)} %get-tuple-element.423) | copy-start | bytes 12582916 | tf_op jit(solution)/shard_map/while
  106.3 4.1 %copy-start.2 = (f32[2,256,2048]{1,2,0:T(8,128)S(1)}, f32[2,256,2048]{1,2,0:T(8,128)}, u32[]{:S(2)}) copy-start(f32[2,256,2048]{1,2,0:T(8,128)} %get-tuple-element.423) | copy-start | bytes 12582916 | tf_op jit(solution)/shard_map/while
  110.4 3.1 %copy-start.4 = (bf16[2048,256]{1,0:T(8,128)(2,1)S(1)}, bf16[2048,256]{1,0:T(8,128)(2,1)}, u32[]{:S(2)}) copy-start(bf16[2048,256]{1,0:T(8,128)(2,1)} %copy-done.3) | copy-start | bytes 3145732 | tf_op jit(solution)/shard_map/while
  113.5 9.1 %copy-start.3 = (bf16[2048,256]{1,0:T(8,128)(2,1)}, bf16[2048,256]{1,0:T(8,128)(2,1)S(1)}, u32[]{:S(2)}) copy-start(bf16[2048,256]{1,0:T(8,128)(2,1)S(1)} %get-tuple-element.475) | copy-start | bytes 3145732 | tf_op jit(solution)/shard_map/while
  123.2 3.9 %copy-start.1 = (f32[2,256,2048]{1,2,0:T(8,128)S(1)}, f32[2,256,2048]{1,2,0:T(8,128)}, u32[]{:S(2)}) copy-start(f32[2,256,2048]{1,2,0:T(8,128)} %get-tuple-element.423) | copy-start | bytes 12582916 | tf_op jit(solution)/shard_map/while
  131.0 4.1 %copy-start.2 = (f32[2,256,2048]{1,2,0:T(8,128)S(1)}, f32[2,256,2048]{1,2,0:T(8,128)}, u32[]{:S(2)}) copy-start(f32[2,256,2048]{1,2,0:T(8,128)} %get-tuple-element.423) | copy-start | bytes 12582916 | tf_op jit(solution)/shard_map/while
  135.1 3.1 %copy-start.4 = (bf16[2048,256]{1,0:T(8,128)(2,1)S(1)}, bf16[2048,256]{1,0:T(8,128)(2,1)}, u32[]{:S(2)}) copy-start(bf16[2048,256]{1,0:T(8,128)(2,1)} %copy-done.3) | copy-start | bytes 3145732 | tf_op jit(solution)/shard_map/while
  138.2 9.1 %copy-start.3 = (bf16[2048,256]{1,0:T(8,128)(2,1)}, bf16[2048,256]{1,0:T(8,128)(2,1)S(1)}, u32[]{:S(2)}) copy-start(bf16[2048,256]{1,0:T(8,128)(2,1)S(1)} %get-tuple-element.475) | copy-start | bytes 3145732 | tf_op jit(solution)/shard_map/while
  147.9 3.9 %copy-start.1 = (f32[2,256,2048]{1,2,0:T(8,128)S(1)}, f32[2,256,2048]{1,2,0:T(8,128)}, u32[]{:S(2)}) copy-start(f32[2,256,2048]{1,2,0:T(8,128)} %get-tuple-element.423) | copy-start | bytes 12582916 | tf_op jit(solution)/shard_map/while
  155.7 4.1 %copy-start.2 = (f32[2,256,2048]{1,2,0:T(8,128)S(1)}, f32[2,256,2048]{1,2,0:T(8,128)}, u32[]{:S(2)}) copy-start(f32[2,256,2048]{1,2,0:T(8,128)} %get-tuple-element.423) | copy-start | bytes 12582916 | tf_op jit(solution)/shard_map/while
  159.8 3.1 %copy-start.4 = (bf16[2048,256]{1,0:T(8,128)(2,1)S(1)}, bf16[2048,256]{1,0:T(8,128)(2,1)}, u32[]{:S(2)}) copy-start(bf16[2048,256]{1,0:T(8,128)(2,1)} %copy-done.3) | copy-start | bytes 3145732 | tf_op jit(solution)/shard_map/while
  164.6 9.0 %collective-permute-start.13 = (bf16[256,256]{1,0:T(8,128)(2,1)S(1)}, bf16[256,256]{1,0:T(8,128)(2,1)S(1)}, u32[]{:S(2)}, u32[]{:S(2)}) collective-permute-start(bf16[256,256]{1,0:T(8,128)(2,1)S(1)} %get-tuple-element.342), channel_id=1, source_target_pairs={{56,0},{64,8},{72,16},{80,24},{88,32},{96,40},{104,48},{112,56},{1... | collective-permute-start | bytes 393224 | tf_op jit(solution)/shard_map/ppermute | solution.py:15
  165.9 10.5 %collective-permute-start.12 = (bf16[256,256]{1,0:T(8,128)(2,1)S(1)}, bf16[256,256]{1,0:T(8,128)(2,1)S(1)}, u32[]{:S(2)}, u32[]{:S(2)}) collective-permute-start(bf16[256,256]{1,0:T(8,128)(2,1)S(1)} %get-tuple-element.343), channel_id=1, source_target_pairs={{48,0},{56,8},{64,16},{72,24},{80,32},{88,40},{96,48},{104,56},{11... | collective-permute-start | bytes 393224 | tf_op jit(solution)/shard_map/ppermute | solution.py:15
  167.9 12.7 %collective-permute-start.11 = (bf16[256,256]{1,0:T(8,128)(2,1)S(1)}, bf16[256,256]{1,0:T(8,128)(2,1)S(1)}, u32[]{:S(2)}, u32[]{:S(2)}) collective-permute-start(bf16[256,256]{1,0:T(8,128)(2,1)S(1)} %get-tuple-element.344), channel_id=1, source_target_pairs={{40,0},{48,8},{56,16},{64,24},{72,32},{80,40},{88,48},{96,56},{104... | collective-permute-start | bytes 393224 | tf_op jit(solution)/shard_map/ppermute | solution.py:15
  169.8 13.4 %collective-permute-start.10 = (bf16[256,256]{1,0:T(8,128)(2,1)S(1)}, bf16[256,256]{1,0:T(8,128)(2,1)S(1)}, u32[]{:S(2)}, u32[]{:S(2)}) collective-permute-start(bf16[256,256]{1,0:T(8,128)(2,1)S(1)} %get-tuple-element.345), channel_id=1, source_target_pairs={{32,0},{40,8},{48,16},{56,24},{64,32},{72,40},{80,48},{88,56},{96,... | collective-permute-start | bytes 393224 | tf_op jit(solution)/shard_map/ppermute | solution.py:15
  171.7 13.3 %collective-permute-start.9 = (bf16[256,256]{1,0:T(8,128)(2,1)S(1)}, bf16[256,256]{1,0:T(8,128)(2,1)S(1)}, u32[]{:S(2)}, u32[]{:S(2)}) collective-permute-start(bf16[256,256]{1,0:T(8,128)(2,1)S(1)} %get-tuple-element.346), channel_id=1, source_target_pairs={{24,0},{32,8},{40,16},{48,24},{56,32},{64,40},{72,48},{80,56},{88,... | collective-permute-start | bytes 393224 | tf_op jit(solution)/shard_map/ppermute | solution.py:15
  173.7 14.9 %collective-permute-start.8 = (bf16[256,256]{1,0:T(8,128)(2,1)S(1)}, bf16[256,256]{1,0:T(8,128)(2,1)S(1)}, u32[]{:S(2)}, u32[]{:S(2)}) collective-permute-start(bf16[256,256]{1,0:T(8,128)(2,1)S(1)} %get-tuple-element.347), channel_id=1, source_target_pairs={{16,0},{24,8},{32,16},{40,24},{48,32},{56,40},{64,48},{72,56},{80,... | collective-permute-start | bytes 393224 | tf_op jit(solution)/shard_map/ppermute | solution.py:15
  176.5 12.2 %collective-permute-start.7 = (bf16[256,256]{1,0:T(8,128)(2,1)S(1)}, bf16[256,256]{1,0:T(8,128)(2,1)S(1)}, u32[]{:S(2)}, u32[]{:S(2)}) collective-permute-start(bf16[256,256]{1,0:T(8,128)(2,1)S(1)} %get-tuple-element.341), channel_id=1, source_target_pairs={{8,0},{16,8},{24,16},{32,24},{40,32},{48,40},{56,48},{64,56},{72,6... | collective-permute-start | bytes 393224 | tf_op jit(solution)/shard_map/ppermute | solution.py:15
  201.7 11.7 %all-to-all-start.3 = ((bf16[8,32,128]{2,1,0:T(8,128)(2,1)}), bf16[8,32,128]{2,1,0:T(8,128)(2,1)S(1)}, u32[]{:S(2)}, u32[]{:S(2)}) async-start(bf16[8,32,128]{2,1,0:T(8,128)(2,1)} %bitcast.16), calls=%async_computation.3 | async-start | bytes 131072 | tf_op jit(solution)/shard_map/all_to_all | solution.py:154
where the time goes:
time: 216 us; the launch traced here: 214 us
  matrix products  63 us (29%)
  starting transfers between devices  57.5 us (27%)
  waiting for transfers between devices  32.5 us (15%)
  local copies, waits for them, and re-layouts  27.4 us (13%)
  other arithmetic  20.8 us (10%)
  blocking collectives  11.3 us (5%)
    ppermute x14, starting transfers between devices, shifted(): lax.ppermute(value, axis, [(source, source + steps) for source in range(l...  43.7 us
    dot_general x4, matrix products, attend_block(): jnp.einsum('htk,kd->thd', weights_low, value_block, preferred_element_typ...  15.4 us
    dot_general x4, matrix products, attend_block(): jnp.einsum('htk,thd->kd', grad_scores, block_q, preferred_element_type=jn...  13.6 us
    dot_general x4, matrix products, attend_block(): jnp.einsum('htk,thd->kd', weights_low, block_g, preferred_element_type=jn...  12.3 us
    ppermute x14, waiting for transfers between devices, shifted(): lax.ppermute(value, axis, [(source, source + steps) for source in range(l...  11.5 us
    all_to_all x1, blocking collectives, body(): lax.all_to_all(grad_k_heads, 'tp', split_axis=0, concat_axis=1, tiled=True)  11.3 us
    reduce_sum x4, other arithmetic, attend_block(): row_total = jnp.sum(jnp.exp(scores - row_top), axis=2, keepdims=True)  11 us
    dot_general x4, matrix products, attend_block(): jnp.einsum('thd,kd->htk', block_q, key_block, preferred_element_type=jnp....  10.7 us
  transfers between devices with their start and end apart: 17, of which 8 were waited for; matrix products, arithmetic and copies ran while one was open for 2% of the time, Pallas kernels for 0%

commit v1 on v0

v1 whole, which is shorter than its diff:
```python
import functools, math
import jax, jax.numpy as jnp
from jax import lax
from jax.sharding import PartitionSpec as P
from jax.experimental import pallas as pl
from jax.experimental.pallas import tpu as pltpu
D=128; T=256; W=8; H=8
SCALE=1.0/math.sqrt(D)
C2=SCALE*math.log2(math.e)
BIG=1e30
NT=(((1,),(1,)),((),()))
f32=jnp.float32; bf16=jnp.bfloat16

def doc_rows(lens_ref):
    sub=lax.broadcasted_iota(jnp.int32,(128,128),0); lane=lax.broadcasted_iota(jnp.int32,(128,128),1)
    lens=jnp.broadcast_to(lens_ref[...],(128,128))
    st=jnp.sum(jnp.where(lane<sub,lens,0.0),axis=1,keepdims=True)
    en=jnp.sum(jnp.where(lane<=sub,lens,0.0),axis=1,keepdims=True)
    st=jnp.transpose(jnp.broadcast_to(st,(128,128)))
    en=jnp.transpose(jnp.broadcast_to(en,(128,128)))
    last=lane==127
    st=jnp.where(last,-1e9,st); en=jnp.where(last,0.0,en)
    return st[0:1],en[0:1]

def attn_kernel(pos_ref,lens_ref,q_ref,g_ref,k_ref,v_ref,o_ref,dq_ref,dk_ref,dv_ref,
                kp,kT,vp,vT,qp,gp,s_ref,p_ref,dk_acc,dv_acc):
    first=pos_ref[0].astype(f32)
    lo,hi=doc_rows(lens_ref)
    sub=lax.broadcasted_iota(jnp.int32,(T,D),0).astype(f32)
    lane=lax.broadcasted_iota(jnp.int32,(T,D),1)
    qpos=first+sub
    qp[:,D:]=jnp.where((qpos>=lo)&(qpos<hi),0.0,-BIG).astype(bf16)
    three=jnp.where(lane<3,1.0,0.0).astype(bf16)
    for j in range(W):
        rows=slice(j*T,(j+1)*T)
        kpos=qpos-j*T
        kp[rows,:D]=k_ref[rows]
        kp[rows,D:]=jnp.where((kpos>=lo)&(kpos<hi),1.0,0.0).astype(bf16)
        vp[rows,:D]=v_ref[rows]
        vp[rows,D:]=three
        kT[:,rows]=jnp.transpose(k_ref[rows])
        vT[:D,rows]=jnp.transpose(v_ref[rows])
        vT[D:,rows]=jnp.ones((16,T),bf16)
    dk_acc[...]=jnp.zeros_like(dk_acc)
    dv_acc[...]=jnp.zeros_like(dv_acc)
    def head(h,_):
        col=pl.ds(pl.multiple_of(h*D,D),D)
        qh=q_ref[:,col]; gh=g_ref[:,col]
        qp[:,:D]=qh
        m=None
        for j in range(W):
            rows=slice(j*T,(j+1)*T)
            s=lax.dot_general(kp[rows],qp[...],NT,preferred_element_type=f32)
            if j==0:
                r=lax.broadcasted_iota(jnp.int32,(T,T),0); c=lax.broadcasted_iota(jnp.int32,(T,T),1)
                s=jnp.where(r<=c,s,-BIG)
            s_ref[rows]=s
            mj=jnp.max(s,axis=0,keepdims=True)
            m=mj if m is None else jnp.maximum(m,mj)
        mc=m*C2
        ot=None
        for j in range(W):
            rows=slice(j*T,(j+1)*T)
            pb=jnp.exp2(s_ref[rows]*C2-mc).astype(bf16)
            p_ref[rows]=pb
            x=jnp.dot(vT[:,rows],pb,preferred_element_type=f32)
            ot=x if ot is None else ot+x
        o=jnp.transpose(ot[:D])
        l=jnp.transpose(ot[D:D+8])[:,0:1]
        inv=1.0/l
        ob=(o*inv).astype(bf16)
        o_ref[:,col]=ob
        gf=gh.astype(f32)
        delta=jnp.sum(ob.astype(f32)*gf,axis=1,keepdims=True)
        rs=inv*SCALE
        g2=(gf*rs).astype(bf16)
        dl=-delta*rs
        d1=dl.astype(bf16).astype(f32); r1=dl-d1
        d2=r1.astype(bf16).astype(f32); d3=r1-d2
        gp[:,:D]=g2
        gp[:,D:]=jnp.where(lane==0,d1,jnp.where(lane==1,d2,jnp.where(lane==2,d3,0.0))).astype(bf16)
        dqt=None
        for j in range(W):
            rows=slice(j*T,(j+1)*T)
            dp=lax.dot_general(vp[rows],gp[...],NT,preferred_element_type=f32)
            pb=p_ref[rows]
            ds=(pb.astype(f32)*dp).astype(bf16)
            dv_acc[rows]+=jnp.dot(pb,g2,preferred_element_type=f32)
            dk_acc[rows]+=jnp.dot(ds,qh,preferred_element_type=f32)
            x=jnp.dot(kT[:,rows],ds,preferred_element_type=f32)
            dqt=x if dqt is None else dqt+x
        dq_ref[:,col]=jnp.transpose(dqt).astype(bf16)
        return 0
    lax.fori_loop(0,H,head,0)
    dk_ref[...]=dk_acc[...].astype(bf16)
    dv_ref[...]=(dv_acc[...]*(1.0/SCALE)).astype(bf16)

def attn(pos,lens,q,g,k,v):
    vm=pl.BlockSpec(memory_space=pltpu.VMEM)
    return pl.pallas_call(attn_kernel,
        out_shape=(jax.ShapeDtypeStruct((T,H*D),bf16),jax.ShapeDtypeStruct((T,H*D),bf16),
                   jax.ShapeDtypeStruct((W*T,D),bf16),jax.ShapeDtypeStruct((W*T,D),bf16)),
        in_specs=[pl.BlockSpec(memory_space=pltpu.SMEM)]+[vm]*5, out_specs=(vm,)*4,
        scratch_shapes=[pltpu.VMEM((W*T,2*D),bf16),pltpu.VMEM((D,W*T),bf16),pltpu.VMEM((W*T,2*D),bf16),pltpu.VMEM((D+16,W*T),bf16),
                        pltpu.VMEM((T,2*D),bf16),pltpu.VMEM((T,2*D),bf16),pltpu.VMEM((W*T,T),f32),pltpu.VMEM((W*T,T),bf16),
                        pltpu.VMEM((W*T,D),f32),pltpu.VMEM((W*T,D),f32)],
        name="attn")(pos,lens,q,g,k,v)


WINDOW = 8


def shifted(value, axis, steps):
    count = lax.axis_size(axis)
    leading, last = (max(0, -steps), min(count, count - steps))
    return lax.ppermute(value, axis, [(source, source + steps) for source in range(leading, last)])


def body(queries, key_vectors, value_vectors, output_gradient, doc_lengths):
    ctx_index = lax.axis_index("ctx")
    k_heads, v_heads = (
        lax.all_to_all(key_vectors, "tp", split_axis=1, concat_axis=0, tiled=True),
        lax.all_to_all(value_vectors, "tp", split_axis=1, concat_axis=0, tiled=True),
    )
    kv_local = jnp.concatenate([k_heads, v_heads], axis=1)
    slots = [kv_local] + [shifted(kv_local, "ctx", j) for j in range(1, WINDOW)]
    window = jnp.concatenate(slots, axis=0)
    lens = jnp.pad(doc_lengths.astype(f32).reshape(1, -1), ((0, 0), (0, 128 - doc_lengths.shape[0])))
    pos = (ctx_index * T).astype(jnp.int32).reshape(1)
    out, dq, dk, dv = attn(pos, lens, queries, output_gradient, window[:, :D], window[:, D:])
    grads = jnp.concatenate([dk, dv], axis=1).reshape(WINDOW, T, 2 * D)
    own = grads[0].astype(f32)
    for j in range(1, WINDOW):
        own = own + shifted(grads[j], "ctx", -j).astype(f32)
    own = own.astype(bf16)
    dkg = lax.all_to_all(own[:, :D], "tp", split_axis=0, concat_axis=1, tiled=True)
    dvg = lax.all_to_all(own[:, D:], "tp", split_axis=0, concat_axis=1, tiled=True)
    return out, dq, dkg, dvg


def solution(mesh):
    return jax.shard_map(
        body,
        mesh=mesh,
        in_specs=(P("ctx", "tp"), P(("ctx", "tp"), None), P(("ctx", "tp"), None), P("ctx", "tp"), P()),
        out_specs=(P("ctx", "tp"), P("ctx", "tp"), P(("ctx", "tp"), None), P(("ctx", "tp"), None)),
        check_vma=False,
    )
```

time: 216 us -> 145 us (0.67)
  the two profiles are of different devices: /device:TPU:6 before, /device:TPU:198 now
where the time goes in v1:
time: 145 us; the launch traced here: 144 us
  starting transfers between devices  59.9 us (41%)
  Pallas kernels  28 us (19%)
  waiting for transfers between devices  27.1 us (19%)
  blocking collectives  21.5 us (15%)
  local copies, waits for them, and re-layouts  6.48 us (4%)
    ppermute x14, starting transfers between devices, shifted(): lax.ppermute(value, axis, [(source, source + steps) for source in range(l...  49.3 us
    pallas_call x1, Pallas kernels, attn(): pl.pallas_call(attn_kernel, out_shape=(jax.ShapeDtypeStruct((T, H * D), b...  28 us
    ppermute x14, waiting for transfers between devices, shifted(): lax.ppermute(value, axis, [(source, source + steps) for source in range(l...  11 us
    all_to_all x1, blocking collectives, body(): lax.all_to_all(value_vectors, 'tp', split_axis=1, concat_axis=0, tiled=True)  10.7 us
    all_to_all x1, blocking collectives, body(): lax.all_to_all(own[:, :D], 'tp', split_axis=0, concat_axis=1, tiled=True)  10.7 us
    all_to_all x1, waiting for transfers between devices, body(): lax.all_to_all(key_vectors, 'tp', split_axis=1, concat_axis=0, tiled=True)  8.35 us
    all_to_all x1, waiting for transfers between devices, body(): lax.all_to_all(own[:, D:], 'tp', split_axis=0, concat_axis=1, tiled=True)  7.66 us
    all_to_all x1, starting transfers between devices, body(): lax.all_to_all(key_vectors, 'tp', split_axis=1, concat_axis=0, tiled=True)  7.23 us
  transfers between devices with their start and end apart: 16, of which 6 were waited for; matrix products, arithmetic and copies ran while one was open for 1% of the time, Pallas kernels for 0%

profile of v1, /device:TPU:198, one launch (start us, length us, event | category | flops | bytes accessed | tf_op | source)
XLA Modules:
  0.0 144.0 jit_solution(3545141279482585111)
XLA Ops:
  0.6 0.0 copy-start
  0.6 0.8 copy-done
  1.5 0.6 copy_bitcast_fusion.3
  2.1 0.0 copy-start.2
  2.1 7.2 %all-to-all-start = ((bf16[32,8,128]{2,0,1:T(8,128)(2,1)}), bf16[32,8,128]{2,0,1:T(8,128)(2,1)S(1)}, u32[]{:S(2)}, u32[]{:S(2)}) async-start(bf16[32,8,128]{2,0,1:T(8,128)(2,1)} %copy_bitcast_fusion.3), calls=%async_computation | async-start | bytes 131072 | tf_op jit(solution)/shard_map/all_to_all | solution.py:122
  9.4 0.0 copy-done.2
  9.4 8.4 %all-to-all-done = bf16[32,8,128]{2,0,1:T(8,128)(2,1)S(1)} async-done(((bf16[32,8,128]{2,0,1:T(8,128)(2,1)}), bf16[32,8,128]{2,0,1:T(8,128)(2,1)S(1)}, u32[]{:S(2)}, u32[]{:S(2)}) %all-to-all-start) | async-done | bytes 65568 | tf_op jit(solution)/shard_map/all_to_all | solution.py:122
  17.7 10.7 %all_to_all.76 = bf16[32,8,128]{2,0,1:T(8,128)(2,1)S(1)} all-to-all(bf16[32,8,128]{2,0,1:T(8,128)(2,1)S(1)} %copy_bitcast_fusion.2), channel_id=1, replica_groups=mesh['ctx'=64,'tp'=8] {'tp'}, dimensions={1} | all-to-all | bytes 131072 | tf_op jit(solution)/shard_map/all_to_all | solution.py:123
  28.5 0.0 copy-start.3
  28.5 5.4 %collective-permute-start.1 = (bf16[256,256]{1,0:T(8,128)(2,1)S(1)}, bf16[256,256]{1,0:T(8,128)(2,1)S(1)}, u32[]{:S(2)}, u32[]{:S(2)}) collective-permute-start(bf16[256,256]{1,0:T(8,128)(2,1)S(1)} %get-tuple-element.23), channel_id=1, source_target_pairs={{0,16},{8,24},{16,32},{24,40},{32,48},{40,56},{48,64},{56,72},{64,... | collective-permute-start | bytes 393224 | tf_op jit(solution)/shard_map/ppermute | solution.py:116
  33.9 1.9 %collective-permute-start = (bf16[256,256]{1,0:T(8,128)(2,1)S(1)}, bf16[256,256]{1,0:T(8,128)(2,1)S(1)}, u32[]{:S(2)}, u32[]{:S(2)}) collective-permute-start(bf16[256,256]{1,0:T(8,128)(2,1)S(1)} %get-tuple-element.23), channel_id=1, source_target_pairs={{0,8},{8,16},{16,24},{24,32},{32,40},{40,48},{48,56},{56,64},{64,7... | collective-permute-start | bytes 393224 | tf_op jit(solution)/shard_map/ppermute | solution.py:116
  35.8 0.0 copy-done.3
  35.9 0.5 pad.4.lens_ref
  36.4 3.4 %collective-permute-start.5 = (bf16[256,256]{1,0:T(8,128)(2,1)S(1)}, bf16[256,256]{1,0:T(8,128)(2,1)S(1)}, u32[]{:S(2)}, u32[]{:S(2)}) collective-permute-start(bf16[256,256]{1,0:T(8,128)(2,1)S(1)} %get-tuple-element.23), channel_id=1, source_target_pairs={{0,48},{8,56},{16,64},{24,72},{32,80},{40,88},{48,96},{56,104},{64... | collective-permute-start | bytes 393224 | tf_op jit(solution)/shard_map/ppermute | solution.py:116
  39.8 5.1 %collective-permute-start.4 = (bf16[256,256]{1,0:T(8,128)(2,1)S(1)}, bf16[256,256]{1,0:T(8,128)(2,1)S(1)}, u32[]{:S(2)}, u32[]{:S(2)}) collective-permute-start(bf16[256,256]{1,0:T(8,128)(2,1)S(1)} %get-tuple-element.23), channel_id=1, source_target_pairs={{0,40},{8,48},{16,56},{24,64},{32,72},{40,80},{48,88},{56,96},{64,... | collective-permute-start | bytes 393224 | tf_op jit(solution)/shard_map/ppermute | solution.py:116
  45.0 3.9 %collective-permute-start.3 = (bf16[256,256]{1,0:T(8,128)(2,1)S(1)}, bf16[256,256]{1,0:T(8,128)(2,1)S(1)}, u32[]{:S(2)}, u32[]{:S(2)}) collective-permute-start(bf16[256,256]{1,0:T(8,128)(2,1)S(1)} %get-tuple-element.23), channel_id=1, source_target_pairs={{0,32},{8,40},{16,48},{24,56},{32,64},{40,72},{48,80},{56,88},{64,... | collective-permute-start | bytes 393224 | tf_op jit(solution)/shard_map/ppermute | solution.py:116
  48.9 0.0 collective-permute-done
  48.9 1.9 %collective-permute-start.2 = (bf16[256,256]{1,0:T(8,128)(2,1)S(1)}, bf16[256,256]{1,0:T(8,128)(2,1)S(1)}, u32[]{:S(2)}, u32[]{:S(2)}) collective-permute-start(bf16[256,256]{1,0:T(8,128)(2,1)S(1)} %get-tuple-element.23), channel_id=1, source_target_pairs={{0,24},{8,32},{16,40},{24,48},{32,56},{40,64},{48,72},{56,80},{64,... | collective-permute-start | bytes 393224 | tf_op jit(solution)/shard_map/ppermute | solution.py:116
  50.9 0.0 collective-permute-done.1
  50.9 6.1 %collective-permute-start.6 = (bf16[256,256]{1,0:T(8,128)(2,1)S(1)}, bf16[256,256]{1,0:T(8,128)(2,1)S(1)}, u32[]{:S(2)}, u32[]{:S(2)}) collective-permute-start(bf16[256,256]{1,0:T(8,128)(2,1)S(1)} %get-tuple-element.23), channel_id=1, source_target_pairs={{0,56},{8,64},{16,72},{24,80},{32,88},{40,96},{48,104},{56,112},{6... | collective-permute-start | bytes 393224 | tf_op jit(solution)/shard_map/ppermute | solution.py:116
  57.0 0.0 collective-permute-done.2
  57.0 0.0 collective-permute-done.3
  57.1 0.0 collective-permute-done.4
  57.1 0.0 collective-permute-done.5
  57.1 2.4 %collective-permute-done.6 = bf16[256,256]{1,0:T(8,128)(2,1)S(1)} collective-permute-done((bf16[256,256]{1,0:T(8,128)(2,1)S(1)}, bf16[256,256]{1,0:T(8,128)(2,1)S(1)}, u32[]{:S(2)}, u32[]{:S(2)}) %collective-permute-start.6) | collective-permute-done | bytes 131104 | tf_op jit(solution)/shard_map/ppermute | solution.py:116
  59.5 1.1 fusion.1
  60.6 28.0 %attn.1 = (bf16[256,1024]{1,0:T(8,128)(2,1)}, bf16[256,1024]{1,0:T(8,128)(2,1)}, bf16[2048,128]{1,0:T(8,128)(2,1)}, bf16[2048,128]{1,0:T(8,128)(2,1)}) custom-call(s32[1]{0:T(128)} %bitcast.pos_ref, f32[1,128]{1,0:T(1,128)} %pad.4.lens_ref, bf16[256,1024]{1,0:T(8,128)(2,1)} %q_ref.1, bf16[256,1024]{1,0:T(8,128)(2,1)} %g_ref.1, ...), custom_call_target="tpu_custom_call" | custom-call | tf_op jit(solution)/shard_map/attn/pallas_call | solution.py:100
  88.6 0.0 copy-start.1
  88.6 1.2 constant_dynamic-update-slice_fusion.9
  89.8 0.0 copy-done.1
  89.8 0.1 constant_dynamic-update-slice_fusion.8
  89.9 0.1 fusion
  90.0 3.8 %collective-permute-start.7 = (bf16[256,256]{1,0:T(8,128)(2,1)S(1)}, bf16[256,256]{1,0:T(8,128)(2,1)S(1)}, u32[]{:S(2)}, u32[]{:S(2)}) collective-permute-start(bf16[256,256]{1,0:T(8,128)(2,1)S(1)} %get-tuple-element.12), channel_id=1, source_target_pairs={{8,0},{16,8},{24,16},{32,24},{40,32},{48,40},{56,48},{64,56},{72,6... | collective-permute-start | bytes 393224 | tf_op jit(solution)/shard_map/ppermute | solution.py:116
  93.8 1.9 %collective-permute-start.13 = (bf16[256,256]{1,0:T(8,128)(2,1)S(1)}, bf16[256,256]{1,0:T(8,128)(2,1)S(1)}, u32[]{:S(2)}, u32[]{:S(2)}) collective-permute-start(bf16[256,256]{1,0:T(8,128)(2,1)S(1)} %get-tuple-element.13), channel_id=1, source_target_pairs={{56,0},{64,8},{72,16},{80,24},{88,32},{96,40},{104,48},{112,56},{1... | collective-permute-start | bytes 393224 | tf_op jit(solution)/shard_map/ppermute | solution.py:116
  95.7 4.3 %collective-permute-start.12 = (bf16[256,256]{1,0:T(8,128)(2,1)S(1)}, bf16[256,256]{1,0:T(8,128)(2,1)S(1)}, u32[]{:S(2)}, u32[]{:S(2)}) collective-permute-start(bf16[256,256]{1,0:T(8,128)(2,1)S(1)} %get-tuple-element.14), channel_id=1, source_target_pairs={{48,0},{56,8},{64,16},{72,24},{80,32},{88,40},{96,48},{104,56},{11... | collective-permute-start | bytes 393224 | tf_op jit(solution)/shard_map/ppermute | solution.py:116
  100.0 1.9 %collective-permute-start.11 = (bf16[256,256]{1,0:T(8,128)(2,1)S(1)}, bf16[256,256]{1,0:T(8,128)(2,1)S(1)}, u32[]{:S(2)}, u32[]{:S(2)}) collective-permute-start(bf16[256,256]{1,0:T(8,128)(2,1)S(1)} %get-tuple-element.15), channel_id=1, source_target_pairs={{40,0},{48,8},{56,16},{64,24},{72,32},{80,40},{88,48},{96,56},{104... | collective-permute-start | bytes 393224 | tf_op jit(solution)/shard_map/ppermute | solution.py:116
  101.9 3.3 %collective-permute-start.10 = (bf16[256,256]{1,0:T(8,128)(2,1)S(1)}, bf16[256,256]{1,0:T(8,128)(2,1)S(1)}, u32[]{:S(2)}, u32[]{:S(2)}) collective-permute-start(bf16[256,256]{1,0:T(8,128)(2,1)S(1)} %get-tuple-element.16), channel_id=1, source_target_pairs={{32,0},{40,8},{48,16},{56,24},{64,32},{72,40},{80,48},{88,56},{96,... | collective-permute-start | bytes 393224 | tf_op jit(solution)/shard_map/ppermute | solution.py:116
  105.2 0.0 collective-permute-done.7
  105.3 3.8 %collective-permute-start.9 = (bf16[256,256]{1,0:T(8,128)(2,1)S(1)}, bf16[256,256]{1,0:T(8,128)(2,1)S(1)}, u32[]{:S(2)}, u32[]{:S(2)}) collective-permute-start(bf16[256,256]{1,0:T(8,128)(2,1)S(1)} %get-tuple-element.17), channel_id=1, source_target_pairs={{24,0},{32,8},{40,16},{48,24},{56,32},{64,40},{72,48},{80,56},{88,... | collective-permute-start | bytes 393224 | tf_op jit(solution)/shard_map/ppermute | solution.py:116
  109.0 0.0 collective-permute-done.13
  109.0 2.5 %collective-permute-start.8 = (bf16[256,256]{1,0:T(8,128)(2,1)S(1)}, bf16[256,256]{1,0:T(8,128)(2,1)S(1)}, u32[]{:S(2)}, u32[]{:S(2)}) collective-permute-start(bf16[256,256]{1,0:T(8,128)(2,1)S(1)} %get-tuple-element.18), channel_id=1, source_target_pairs={{16,0},{24,8},{32,16},{40,24},{48,32},{56,40},{64,48},{72,56},{80,... | collective-permute-start | bytes 393224 | tf_op jit(solution)/shard_map/ppermute | solution.py:116
  111.5 0.0 collective-permute-done.12
  111.5 0.0 collective-permute-done.11
  111.5 3.1 %collective-permute-done.10 = bf16[256,256]{1,0:T(8,128)(2,1)S(1)} collective-permute-done((bf16[256,256]{1,0:T(8,128)(2,1)S(1)}, bf16[256,256]{1,0:T(8,128)(2,1)S(1)}, u32[]{:S(2)}, u32[]{:S(2)}) %collective-permute-start.10) | collective-permute-done | bytes 131104 | tf_op jit(solution)/shard_map/ppermute | solution.py:116
  114.6 1.2 collective-permute-done.9
  115.8 4.4 %collective-permute-done.8 = bf16[256,256]{1,0:T(8,128)(2,1)S(1)} collective-permute-done((bf16[256,256]{1,0:T(8,128)(2,1)S(1)}, bf16[256,256]{1,0:T(8,128)(2,1)S(1)}, u32[]{:S(2)}, u32[]{:S(2)}) %collective-permute-start.8) | collective-permute-done | bytes 131104 | tf_op jit(solution)/shard_map/ppermute | solution.py:116
  120.2 0.1 add_convert_fusion
  120.4 0.6 fusion.2
  121.0 10.7 %all_to_all.77 = bf16[8,32,128]{2,1,0:T(8,128)(2,1)S(1)} all-to-all(bf16[8,32,128]{2,1,0:T(8,128)(2,1)S(1)} %bitcast.35), channel_id=1, replica_groups=mesh['ctx'=64,'tp'=8] {'tp'}, dimensions={0} | all-to-all | bytes 131072 | tf_op jit(solution)/shard_map/all_to_all | solution.py:136
  131.7 3.4 %all-to-all-start.3 = ((bf16[8,32,128]{2,1,0:T(8,128)(2,1)}), bf16[8,32,128]{2,1,0:T(8,128)(2,1)S(1)}, u32[]{:S(2)}, u32[]{:S(2)}) async-start(bf16[8,32,128]{2,1,0:T(8,128)(2,1)} %bitcast.8), calls=%async_computation.3 | async-start | bytes 131072 | tf_op jit(solution)/shard_map/all_to_all | solution.py:137
  135.1 0.6 copy_bitcast_fusion.1
  135.7 7.7 %all-to-all-done.3 = bf16[8,32,128]{2,1,0:T(8,128)(2,1)S(1)} async-done(((bf16[8,32,128]{2,1,0:T(8,128)(2,1)}), bf16[8,32,128]{2,1,0:T(8,128)(2,1)S(1)}, u32[]{:S(2)}, u32[]{:S(2)}) %all-to-all-start.3) | async-done | bytes 65568 | tf_op jit(solution)/shard_map/all_to_all | solution.py:137
  143.4 0.6 copy_bitcast_fusion
  (10 shorter events, 0.1 us)
Async XLA Ops:
  0.6 0.8 copy-start
  2.1 7.2 %copy-start.2 = (bf16[32,1024]{1,0:T(8,128)(2,1)S(1)}, bf16[32,1024]{1,0:T(8,128)(2,1)}, u32[]{:S(2)}) copy-start(bf16[32,1024]{1,0:T(8,128)(2,1)} %param.7) | copy-start | bytes 196612
  2.1 15.6 %all-to-all-start = ((bf16[32,8,128]{2,0,1:T(8,128)(2,1)}), bf16[32,8,128]{2,0,1:T(8,128)(2,1)S(1)}, u32[]{:S(2)}, u32[]{:S(2)}) async-start(bf16[32,8,128]{2,0,1:T(8,128)(2,1)} %copy_bitcast_fusion.3), calls=%async_computation | async-start | bytes 131072 | tf_op jit(solution)/shard_map/all_to_all | solution.py:122
  28.5 7.4 %copy-start.3 = (s32[32]{0:T(128)S(1)}, s32[32]{0:T(128)}, u32[]{:S(2)}) copy-start(s32[32]{0:T(128)} %param.9) | copy-start | bytes 388
  28.5 22.4 %collective-permute-start.1 = (bf16[256,256]{1,0:T(8,128)(2,1)S(1)}, bf16[256,256]{1,0:T(8,128)(2,1)S(1)}, u32[]{:S(2)}, u32[]{:S(2)}) collective-permute-start(bf16[256,256]{1,0:T(8,128)(2,1)S(1)} %get-tuple-element.23), channel_id=1, source_target_pairs={{0,16},{8,24},{16,32},{24,40},{32,48},{40,56},{48,64},{56,72},{64,... | collective-permute-start | bytes 393224 | tf_op jit(solution)/shard_map/ppermute | solution.py:116
  33.9 15.0 %collective-permute-start = (bf16[256,256]{1,0:T(8,128)(2,1)S(1)}, bf16[256,256]{1,0:T(8,128)(2,1)S(1)}, u32[]{:S(2)}, u32[]{:S(2)}) collective-permute-start(bf16[256,256]{1,0:T(8,128)(2,1)S(1)} %get-tuple-element.23), channel_id=1, source_target_pairs={{0,8},{8,16},{16,24},{24,32},{32,40},{40,48},{48,56},{56,64},{64,7... | collective-permute-start | bytes 393224 | tf_op jit(solution)/shard_map/ppermute | solution.py:116
  36.4 20.7 %collective-permute-start.5 = (bf16[256,256]{1,0:T(8,128)(2,1)S(1)}, bf16[256,256]{1,0:T(8,128)(2,1)S(1)}, u32[]{:S(2)}, u32[]{:S(2)}) collective-permute-start(bf16[256,256]{1,0:T(8,128)(2,1)S(1)} %get-tuple-element.23), channel_id=1, source_target_pairs={{0,48},{8,56},{16,64},{24,72},{32,80},{40,88},{48,96},{56,104},{64... | collective-permute-start | bytes 393224 | tf_op jit(solution)/shard_map/ppermute | solution.py:116
  39.8 17.2 %collective-permute-start.4 = (bf16[256,256]{1,0:T(8,128)(2,1)S(1)}, bf16[256,256]{1,0:T(8,128)(2,1)S(1)}, u32[]{:S(2)}, u32[]{:S(2)}) collective-permute-start(bf16[256,256]{1,0:T(8,128)(2,1)S(1)} %get-tuple-element.23), channel_id=1, source_target_pairs={{0,40},{8,48},{16,56},{24,64},{32,72},{40,80},{48,88},{56,96},{64,... | collective-permute-start | bytes 393224 | tf_op jit(solution)/shard_map/ppermute | solution.py:116
  45.0 12.1 %collective-permute-start.3 = (bf16[256,256]{1,0:T(8,128)(2,1)S(1)}, bf16[256,256]{1,0:T(8,128)(2,1)S(1)}, u32[]{:S(2)}, u32[]{:S(2)}) collective-permute-start(bf16[256,256]{1,0:T(8,128)(2,1)S(1)} %get-tuple-element.23), channel_id=1, source_target_pairs={{0,32},{8,40},{16,48},{24,56},{32,64},{40,72},{48,80},{56,88},{64,... | collective-permute-start | bytes 393224 | tf_op jit(solution)/shard_map/ppermute | solution.py:116
  48.9 8.1 %collective-permute-start.2 = (bf16[256,256]{1,0:T(8,128)(2,1)S(1)}, bf16[256,256]{1,0:T(8,128)(2,1)S(1)}, u32[]{:S(2)}, u32[]{:S(2)}) collective-permute-start(bf16[256,256]{1,0:T(8,128)(2,1)S(1)} %get-tuple-element.23), channel_id=1, source_target_pairs={{0,24},{8,32},{16,40},{24,48},{32,56},{40,64},{48,72},{56,80},{64,... | collective-permute-start | bytes 393224 | tf_op jit(solution)/shard_map/ppermute | solution.py:116
  50.9 8.6 %collective-permute-start.6 = (bf16[256,256]{1,0:T(8,128)(2,1)S(1)}, bf16[256,256]{1,0:T(8,128)(2,1)S(1)}, u32[]{:S(2)}, u32[]{:S(2)}) collective-permute-start(bf16[256,256]{1,0:T(8,128)(2,1)S(1)} %get-tuple-element.23), channel_id=1, source_target_pairs={{0,56},{8,64},{16,72},{24,80},{32,88},{40,96},{48,104},{56,112},{6... | collective-permute-start | bytes 393224 | tf_op jit(solution)/shard_map/ppermute | solution.py:116
  88.6 1.2 copy-start.1
  90.0 15.2 %collective-permute-start.7 = (bf16[256,256]{1,0:T(8,128)(2,1)S(1)}, bf16[256,256]{1,0:T(8,128)(2,1)S(1)}, u32[]{:S(2)}, u32[]{:S(2)}) collective-permute-start(bf16[256,256]{1,0:T(8,128)(2,1)S(1)} %get-tuple-element.12), channel_id=1, source_target_pairs={{8,0},{16,8},{24,16},{32,24},{40,32},{48,40},{56,48},{64,56},{72,6... | collective-permute-start | bytes 393224 | tf_op jit(solution)/shard_map/ppermute | solution.py:116
  93.8 15.3 %collective-permute-start.13 = (bf16[256,256]{1,0:T(8,128)(2,1)S(1)}, bf16[256,256]{1,0:T(8,128)(2,1)S(1)}, u32[]{:S(2)}, u32[]{:S(2)}) collective-permute-start(bf16[256,256]{1,0:T(8,128)(2,1)S(1)} %get-tuple-element.13), channel_id=1, source_target_pairs={{56,0},{64,8},{72,16},{80,24},{88,32},{96,40},{104,48},{112,56},{1... | collective-permute-start | bytes 393224 | tf_op jit(solution)/shard_map/ppermute | solution.py:116
  95.7 15.8 %collective-permute-start.12 = (bf16[256,256]{1,0:T(8,128)(2,1)S(1)}, bf16[256,256]{1,0:T(8,128)(2,1)S(1)}, u32[]{:S(2)}, u32[]{:S(2)}) collective-permute-start(bf16[256,256]{1,0:T(8,128)(2,1)S(1)} %get-tuple-element.14), channel_id=1, source_target_pairs={{48,0},{56,8},{64,16},{72,24},{80,32},{88,40},{96,48},{104,56},{11... | collective-permute-start | bytes 393224 | tf_op jit(solution)/shard_map/ppermute | solution.py:116
  100.0 11.5 %collective-permute-start.11 = (bf16[256,256]{1,0:T(8,128)(2,1)S(1)}, bf16[256,256]{1,0:T(8,128)(2,1)S(1)}, u32[]{:S(2)}, u32[]{:S(2)}) collective-permute-start(bf16[256,256]{1,0:T(8,128)(2,1)S(1)} %get-tuple-element.15), channel_id=1, source_target_pairs={{40,0},{48,8},{56,16},{64,24},{72,32},{80,40},{88,48},{96,56},{104... | collective-permute-start | bytes 393224 | tf_op jit(solution)/shard_map/ppermute | solution.py:116
  101.9 12.7 %collective-permute-start.10 = (bf16[256,256]{1,0:T(8,128)(2,1)S(1)}, bf16[256,256]{1,0:T(8,128)(2,1)S(1)}, u32[]{:S(2)}, u32[]{:S(2)}) collective-permute-start(bf16[256,256]{1,0:T(8,128)(2,1)S(1)} %get-tuple-element.16), channel_id=1, source_target_pairs={{32,0},{40,8},{48,16},{56,24},{64,32},{72,40},{80,48},{88,56},{96,... | collective-permute-start | bytes 393224 | tf_op jit(solution)/shard_map/ppermute | solution.py:116
  105.3 10.6 %collective-permute-start.9 = (bf16[256,256]{1,0:T(8,128)(2,1)S(1)}, bf16[256,256]{1,0:T(8,128)(2,1)S(1)}, u32[]{:S(2)}, u32[]{:S(2)}) collective-permute-start(bf16[256,256]{1,0:T(8,128)(2,1)S(1)} %get-tuple-element.17), channel_id=1, source_target_pairs={{24,0},{32,8},{40,16},{48,24},{56,32},{64,40},{72,48},{80,56},{88,... | collective-permute-start | bytes 393224 | tf_op jit(solution)/shard_map/ppermute | solution.py:116
  109.0 11.2 %collective-permute-start.8 = (bf16[256,256]{1,0:T(8,128)(2,1)S(1)}, bf16[256,256]{1,0:T(8,128)(2,1)S(1)}, u32[]{:S(2)}, u32[]{:S(2)}) collective-permute-start(bf16[256,256]{1,0:T(8,128)(2,1)S(1)} %get-tuple-element.18), channel_id=1, source_target_pairs={{16,0},{24,8},{32,16},{40,24},{48,32},{56,40},{64,48},{72,56},{80,... | collective-permute-start | bytes 393224 | tf_op jit(solution)/shard_map/ppermute | solution.py:116
  131.7 11.7 %all-to-all-start.3 = ((bf16[8,32,128]{2,1,0:T(8,128)(2,1)}), bf16[8,32,128]{2,1,0:T(8,128)(2,1)S(1)}, u32[]{:S(2)}, u32[]{:S(2)}) async-start(bf16[8,32,128]{2,1,0:T(8,128)(2,1)} %bitcast.8), calls=%async_computation.3 | async-start | bytes 131072 | tf_op jit(solution)/shard_map/all_to_all | solution.py:137

commit v2 on v1

v2 whole, which is shorter than its diff:
```python
import functools
import math

import jax
import jax.numpy as jnp
from jax import lax
from jax.experimental import pallas as pl
from jax.experimental.pallas import tpu as pltpu
from jax.sharding import PartitionSpec as P

D = 128
T = 256
W = 8
H = 8
NX = 4
ND = 8
ROWS = T // ND
SCALE = 1.0 / math.sqrt(D)
C2 = SCALE * math.log2(math.e)
BIG = 1e30
NT = (((1,), (1,)), ((), ()))
f32 = jnp.float32
bf16 = jnp.bfloat16
MESH = pl.DeviceIdType.MESH


ORDER = (7, 5, 6, 3, 4, 1, 2, 0)
KEYS = slice(0, T)
VALUES = slice(T, 2 * T)


def doc_rows(lens_ref):
    n = lens_ref.shape[1]
    sub = lax.broadcasted_iota(jnp.int32, (128, n), 0)
    lane = lax.broadcasted_iota(jnp.int32, (128, n), 1)
    lens = jnp.broadcast_to(lens_ref[...].astype(f32), (128, n))
    st = jnp.sum(jnp.where(lane < sub, lens, 0.0), axis=1, keepdims=True)
    en = jnp.sum(jnp.where(lane <= sub, lens, 0.0), axis=1, keepdims=True)
    st = jnp.transpose(jnp.broadcast_to(st, (128, 128)))
    en = jnp.transpose(jnp.broadcast_to(en, (128, 128)))
    last = lax.broadcasted_iota(jnp.int32, (128, 128), 1) == 127
    st = jnp.where(last, -1e9, st)
    en = jnp.where(last, 0.0, en)
    return st[0:1], en[0:1]


def kernel(
    nctx, lens_ref, q_hbm, g_hbm, k_hbm, v_hbm, o_ref, dq_ref, dk_ref, dv_ref,
    q_ref, g_ref, kv, gb, pst, xst, zst, fin, kg, vg,
    qa, kb, three, qall, g2all, dall, kT, vT, m_ref, s_ref, p_ref, ds_ref,
    lsem, asend, arecv, zsend, zrecv, xsend, xrecv, psend, precv,
):
    i = lax.axis_index("ctx")
    me = lax.axis_index("tp")
    core = lax.rem(i, 2)
    x = lax.rem(lax.div(i, 2), NX)
    row = i - lax.rem(i, 2 * NX)
    base = lax.rem(i, 2 * NX)
    partner = i + 1 - 2 * core
    up = lax.rem(i + 2 * NX, nctx)
    down = lax.rem(i + nctx - 2 * NX, nctx)

    def chip(j):
        return row + lax.rem(base + 2 * j, 2 * NX)

    def peer(d):
        return lax.rem(me + d, ND)

    def remote(src, dst, send, recv, who):
        return pltpu.make_async_remote_copy(
            src_ref=src, dst_ref=dst, send_sem=send, recv_sem=recv, device_id=who, device_id_type=MESH
        )

    own_col = pl.ds(pl.multiple_of(me * D, D), D)
    own_row = [pl.ds(pl.multiple_of(half * T + me * ROWS, ROWS), ROWS) for half in (0, 1)]
    source = (k_hbm, v_hbm)
    loads = [pltpu.make_async_copy(q_hbm, q_ref, lsem.at[0]), pltpu.make_async_copy(g_hbm, g_ref, lsem.at[1])]
    for half in (0, 1):
        loads.append(
            pltpu.make_async_copy(source[half].at[:, own_col], kv.at[0, own_row[half]], lsem.at[2 + half])
        )
    for copy in loads:
        copy.start()

    barrier = pltpu.get_barrier_semaphore()
    greeted = [(i, peer(d)) for d in range(1, ND)]
    greeted += [(c, me) for c in (partner, up, down, chip(1), chip(2), chip(3))]
    for who in greeted:
        pl.semaphore_signal(barrier, inc=1, device_id=who, device_id_type=MESH)
    pl.semaphore_wait(barrier, len(greeted))

    spread = [[], []]
    for half in (0, 1):
        for d in range(1, ND):
            col = pl.ds(pl.multiple_of(peer(d) * D, D), D)
            copy = remote(
                source[half].at[:, col], kv.at[0, own_row[half]], asend.at[half, d], arecv.at[half, d], (i, peer(d))
            )
            copy.start()
            spread[half].append(copy)

    lo, hi = doc_rows(lens_ref)
    pos0 = (i * T).astype(f32)
    sub = lax.broadcasted_iota(jnp.int32, (T, D), 0).astype(f32)
    lane = lax.broadcasted_iota(jnp.int32, (T, D), 1)
    qpos = pos0 + sub
    qa[...] = jnp.where((qpos >= lo) & (qpos < hi), 0.0, -BIG).astype(bf16)
    three[...] = jnp.where(lane < 3, 1.0, 0.0).astype(bf16)
    for j in range(W):
        kpos = qpos - j * T
        kb[j * T : (j + 1) * T] = jnp.where((kpos >= lo) & (kpos < hi), 1.0, 0.0).astype(bf16)
    vT[D:] = jnp.ones((16, W * T), bf16)
    m_ref[...] = jnp.full(m_ref.shape, -3e38, f32)
    loads[0].wait()
    loads[1].wait()
    for h in range(H):
        qall[h * T : (h + 1) * T] = q_ref[:, h * D : (h + 1) * D]

    half_of = (KEYS, VALUES)

    def zcopy(half):
        part = half_of[half]
        return remote(kv.at[0, part], kv.at[8, part], zsend.at[half], zrecv.at[half], (up, me))

    def xcopy(j, half):
        part = half_of[half]
        src = jnp.where(x + j < NX, 0, 8)
        return remote(kv.at[src, part], kv.at[2 * j, part], xsend.at[half, j], xrecv.at[half, j], (chip(j), me))

    def share(m, half):
        part = half_of[half]
        return remote(
            kv.at[2 * (m + core), part], kv.at[2 * m + 1, part], psend.at[half, m], precv.at[half, m], (partner, me)
        )

    for half in (0, 1):
        loads[2 + half].wait()
        for copy in spread[half]:
            copy.wait()
        zcopy(half).start()
        for j in (1, 3, 2):
            pl.when(x + j < NX)(xcopy(j, half).start)
        pl.when(core == 0)(lambda half=half: share(0, half).start())

    def scores(j):
        rows = slice(j * T, (j + 1) * T)
        keys = kv[j, KEYS]
        kT[:, rows] = jnp.transpose(keys)
        left = jnp.concatenate([keys, kb[rows]], axis=1)
        for h in range(H):
            cols = slice(h * T, (h + 1) * T)
            right = jnp.concatenate([qall[cols], qa[...]], axis=1)
            s = lax.dot_general(left, right, NT, preferred_element_type=f32)
            if j == 0:
                r = lax.broadcasted_iota(jnp.int32, (T, T), 0)
                c = lax.broadcasted_iota(jnp.int32, (T, T), 1)
                s = jnp.where(r <= c, s, -BIG)
            s_ref[rows, cols] = s
            m_ref[:, cols] = jnp.maximum(m_ref[:, cols], jnp.max(s.reshape(T // 8, 8, T), axis=0))

    scores(0)
    for half in (0, 1):
        zcopy(half).wait_recv()
        for j in (1, 3, 2):
            pl.when(x + j >= NX)(xcopy(j, half).start)
        pl.when(core == 1)(lambda half=half: share(3, half).start())
    for j in (1, 3, 2):
        xcopy(j, 0).wait_recv()
        share(j - core, 0).start()
        scores(2 * j)
    for j in (1, 3, 2):
        xcopy(j, 1).wait_recv()
        share(j - core, 1).start()
    for m in range(4):
        share(m, 0).wait()
        scores(2 * m + 1)
    for m in range(4):
        share(m, 1).wait()
    for half in (0, 1):
        zcopy(half).wait_send()
        for j in (1, 3, 2):
            xcopy(j, half).wait_send()
    for j in range(W):
        vT[:D, j * T : (j + 1) * T] = jnp.transpose(kv[j, VALUES])

    for h in range(H):
        cols = slice(h * T, (h + 1) * T)
        col = slice(h * D, (h + 1) * D)
        mc = jnp.max(m_ref[:, cols], axis=0, keepdims=True) * C2
        for j in range(W):
            rows = slice(j * T, (j + 1) * T)
            p_ref[rows, cols] = jnp.exp2(s_ref[rows, cols] * C2 - mc).astype(bf16)
        ot = jnp.dot(vT[...], p_ref[:, cols], preferred_element_type=f32)
        o = jnp.transpose(ot[:D])
        total = jnp.transpose(ot[D : D + 8])[:, 0:1]
        inv = 1.0 / total
        ob = (o * inv).astype(bf16)
        o_ref[:, col] = ob
        gf = g_ref[:, col].astype(f32)
        delta = jnp.sum(ob.astype(f32) * gf, axis=1, keepdims=True)
        rs = inv * SCALE
        g2all[cols] = (gf * rs).astype(bf16)
        dl = -delta * rs
        d1 = dl.astype(bf16).astype(f32)
        r1 = dl - d1
        d2 = r1.astype(bf16).astype(f32)
        d3 = r1 - d2
        dall[cols] = jnp.where(lane == 0, d1, jnp.where(lane == 1, d2, jnp.where(lane == 2, d3, 0.0))).astype(bf16)

    def gradients(j):
        rows = slice(j * T, (j + 1) * T)
        left = jnp.concatenate([kv[j, VALUES], three[...]], axis=1)
        dv = jnp.dot(p_ref[rows], g2all[...], preferred_element_type=f32)
        dk = None
        for part in range(2):
            for h in range(part * H // 2, (part + 1) * H // 2):
                cols = slice(h * T, (h + 1) * T)
                right = jnp.concatenate([g2all[cols], dall[cols]], axis=1)
                dp = lax.dot_general(left, right, NT, preferred_element_type=f32)
                ds_ref[rows, cols] = (p_ref[rows, cols].astype(f32) * dp).astype(bf16)
            cols = slice(part * H // 2 * T, (part + 1) * H // 2 * T)
            piece = jnp.dot(ds_ref[rows, cols], qall[cols], preferred_element_type=f32)
            dk = piece if dk is None else dk + piece
        return dk, dv * (1.0 / SCALE)

    def query_gradient(h):
        cols = slice(h * T, (h + 1) * T)
        dqt = jnp.dot(kT[...], ds_ref[:, cols], preferred_element_type=f32)
        dq_ref[:, h * D : (h + 1) * D] = jnp.transpose(dqt).astype(bf16)

    def give(m):
        return remote(gb.at[2 * m + 1], pst.at[m], psend.at[2, m], precv.at[2, m], (partner, me))

    def xback(j, half):
        part = half_of[half]
        return remote(
            gb.at[2 * j, part], xst.at[j, part], xsend.at[2 + half, j], xrecv.at[2 + half, j], (chip(NX - j), me)
        )

    def zback(half):
        part = half_of[half]
        return remote(gb.at[8, part], zst.at[part], zsend.at[2 + half], zrecv.at[2 + half], (down, me))

    own = None
    for j in ORDER:
        dk, dv = gradients(j)
        if j == 0:
            own = [dk, dv]
        elif j % 2:
            gb[j, KEYS] = dk.astype(bf16)
            gb[j, VALUES] = dv.astype(bf16)
            give(j // 2).start()
        else:
            if j == 6:
                give(3).wait()
                give(2).wait()
            elif j == 4:
                give(1).wait()
            else:
                give(0).wait()
            other = pst[j // 2 - core].astype(f32)
            gb[j, KEYS] = (dk + other[:T]).astype(bf16)
            gb[j, VALUES] = (dv + other[T:]).astype(bf16)
            for half in (0, 1):
                xback(j // 2, half).start()

    first_part = jnp.where(core == 0, 1.0, 0.0)
    last_part = jnp.where(core == 1, 1.0, 0.0)
    for h in range(3):
        query_gradient(h)
    prev = [None, None]
    for half in (0, 1):
        part = half_of[half]
        own[half] += pst[0, part].astype(f32) * first_part
        prev[half] = pst[3, part].astype(f32) * last_part
        for j in (3, 2, 1):
            xback(j, half).wait()
            mine = jnp.where(x + j < NX, 1.0, 0.0)
            got = xst[j, part].astype(f32)
            own[half] += got * mine
            prev[half] += got * (1.0 - mine)
        gb[8, part] = prev[half].astype(bf16)
        zback(half).start()
    for h in range(3, 6):
        query_gradient(h)
    out = (kg, vg)
    last = []
    for half in (0, 1):
        part = half_of[half]
        zback(half).wait()
        fin[part] = (own[half] + zst[part].astype(f32)).astype(bf16)
        for d in range(1, ND):
            rows = pl.ds(pl.multiple_of(half * T + peer(d) * ROWS, ROWS), ROWS)
            copy = remote(
                fin.at[rows], out[half].at[:, own_col], asend.at[2 + half, d], arecv.at[2 + half, d], (i, peer(d))
            )
            copy.start()
            last.append(copy)
    for h in range(6, 8):
        query_gradient(h)
    kg[:, own_col] = fin[own_row[0]]
    vg[:, own_col] = fin[own_row[1]]
    for copy in last:
        copy.wait()
    dk_ref[...] = kg[...]
    dv_ref[...] = vg[...]


def write_kernel(o_in, dq_in, dk_in, dv_in, o_out, dq_out, dk_out, dv_out, sem):
    pairs = ((o_in, o_out), (dq_in, dq_out), (dk_in, dk_out), (dv_in, dv_out))
    copies = [pltpu.make_async_copy(a, b, sem.at[n]) for n, (a, b) in enumerate(pairs)]
    for copy in copies:
        copy.start()
    for copy in copies:
        copy.wait()


def body(queries, key_vectors, value_vectors, output_gradient, doc_lengths):
    vm = pl.BlockSpec(memory_space=pltpu.VMEM)
    free = pl.BlockSpec(memory_space=pl.ANY)
    dma = pltpu.SemaphoreType.DMA
    vmem = pltpu.VMEM
    big = jax.ShapeDtypeStruct((T, H * D), bf16)
    small = jax.ShapeDtypeStruct((ROWS, ND * D), bf16)
    arrays = [
        pltpu.with_memory_space_constraint(a, pltpu.HBM)
        for a in (queries, output_gradient, key_vectors, value_vectors)
    ]
    parts = pl.pallas_call(
        functools.partial(kernel, lax.axis_size("ctx")),
        out_shape=(big, big, small, small),
        in_specs=[vm] + [free] * 4,
        out_specs=(vm,) * 4,
        scratch_shapes=[
            vmem((T, H * D), bf16),
            vmem((T, H * D), bf16),
            vmem((9, 2 * T, D), bf16),
            vmem((9, 2 * T, D), bf16),
            vmem((4, 2 * T, D), bf16),
            vmem((4, 2 * T, D), bf16),
            vmem((2 * T, D), bf16),
            vmem((2 * T, D), bf16),
            vmem((ROWS, ND * D), bf16),
            vmem((ROWS, ND * D), bf16),
            vmem((T, D), bf16),
            vmem((W * T, D), bf16),
            vmem((T, D), bf16),
            vmem((H * T, D), bf16),
            vmem((H * T, D), bf16),
            vmem((H * T, D), bf16),
            vmem((D, W * T), bf16),
            vmem((D + 16, W * T), bf16),
            vmem((8, H * T), f32),
            vmem((W * T, H * T), f32),
            vmem((W * T, H * T), bf16),
            vmem((W * T, H * T), bf16),
            dma((4,)),
            dma((4, ND)),
            dma((4, ND)),
            dma((4,)),
            dma((4,)),
            dma((4, NX)),
            dma((4, NX)),
            dma((3, 4)),
            dma((3, 4)),
        ],
        compiler_params=pltpu.CompilerParams(
            collective_id=0, has_side_effects=True, vmem_limit_bytes=52 << 20
        ),
        name="attention",
    )(doc_lengths.reshape(1, -1), *arrays)
    return pl.pallas_call(
        write_kernel,
        out_shape=(big, big, small, small),
        in_specs=[free] * 4,
        out_specs=(free,) * 4,
        scratch_shapes=[dma((4,))],
        compiler_params=pltpu.CompilerParams(vmem_limit_bytes=2 << 20),
        name="write",
    )(*parts)


def solution(mesh):
    return jax.shard_map(
        body,
        mesh=mesh,
        in_specs=(P("ctx", "tp"), P(("ctx", "tp"), None), P(("ctx", "tp"), None), P("ctx", "tp"), P()),
        out_specs=(P("ctx", "tp"), P("ctx", "tp"), P(("ctx", "tp"), None), P(("ctx", "tp"), None)),
        check_vma=False,
    )
```

time: 145 us -> 62.1 us (0.43)
  the two profiles are of different devices: /device:TPU:198 before, /device:TPU:6 now
where the time goes in v2:
time: 62.1 us; the launch traced here: 61.9 us
  Pallas kernels  60.5 us (97%)
  between operations  0.81 us (1%)
  local copies, waits for them, and re-layouts  0.65 us (1%)
    pallas_call x1, Pallas kernels, body(): pl.pallas_call(functools.partial(kernel, lax.axis_size('ctx')), out_shape...  59.4 us

profile of v2, /device:TPU:6, one launch (start us, length us, event | category | flops | bytes accessed | tf_op | source)
XLA Modules:
  0.0 61.9 jit_solution(15748045263814074445)
XLA Ops:
  0.6 0.0 copy-start
  0.6 0.6 %copy-done = s32[32]{0:T(128)S(1)} copy-done((s32[32]{0:T(128)S(1)}, s32[32]{0:T(128)}, u32[]{:S(2)}) %copy-start) | copy-done | bytes 152
  1.3 59.4 %attention.1 = (bf16[256,1024]{1,0:T(8,128)(2,1)S(1)}, bf16[256,1024]{1,0:T(8,128)(2,1)S(1)}, bf16[32,1024]{1,0:T(8,128)(2,1)S(1)}, bf16[32,1024]{1,0:T(8,128)(2,1)S(1)}) custom-call(s32[1,32]{1,0:T(1,128)S(1)} %bitcast.1, bf16[256,1024]{1,0:T(8,128)(2,1)} %q_hbm.1, bf16[256,1024]{1,0:T(8,128)(2,1)} %g_hbm.1, bf16[32,1024]{1,0:T(8,128)(2,1)} %k_hbm.1, ...), custom_call_target="tpu_custom_call" | custom-call | tf_op jit(solution)/shard_map/attention/pallas_call | solution.py:329
  60.7 1.0 %write.1 = (bf16[256,1024]{1,0:T(8,128)(2,1)}, bf16[256,1024]{1,0:T(8,128)(2,1)}, bf16[32,1024]{1,0:T(8,128)(2,1)}, bf16[32,1024]{1,0:T(8,128)(2,1)}) custom-call(bf16[256,1024]{1,0:T(8,128)(2,1)S(1)} %get-tuple-element.8.o_in, bf16[256,1024]{1,0:T(8,128)(2,1)S(1)} %get-tuple-element.9.dq_in, bf16[32,1024]{1,0:T(8,128)(2,1)S(1)} %get-tuple-element.10.dk_in, ...), custom_call_target="tpu_custom_call" | custom-call | tf_op jit(solution)/shard_map/write/pallas_call | solution.py:372
Async XLA Ops:
  0.6 0.7 %copy-start = (s32[32]{0:T(128)S(1)}, s32[32]{0:T(128)}, u32[]{:S(2)}) copy-start(s32[32]{0:T(128)} %param.9) | copy-start | bytes 388

commit v3 on v2

--- a/solution.py
+++ b/solution.py
@@ -24,7 +24,6 @@
 MESH = pl.DeviceIdType.MESH
 
 
-ORDER = (7, 5, 6, 3, 4, 1, 2, 0)
 KEYS = slice(0, T)
 VALUES = slice(T, 2 * T)
 
@@ -46,7 +45,7 @@
 
 def kernel(
     nctx, lens_ref, q_hbm, g_hbm, k_hbm, v_hbm, o_ref, dq_ref, dk_ref, dv_ref,
-    q_ref, g_ref, kv, gb, pst, xst, zst, fin, kg, vg,
+    q_ref, g_ref, kv, gb, pst, xst, zst, own, fin, kg, vg,
     qa, kb, three, qall, g2all, dall, kT, vT, m_ref, s_ref, p_ref, ds_ref,
     lsem, asend, arecv, zsend, zrecv, xsend, xrecv, psend, precv,
 ):
@@ -59,6 +58,9 @@
     partner = i + 1 - 2 * core
     up = lax.rem(i + 2 * NX, nctx)
     down = lax.rem(i + nctx - 2 * NX, nctx)
+    z = lax.div(i, 2 * NX)
+    not_first = z > 0
+    not_last = z < nctx // (2 * NX) - 1
 
     def chip(j):
         return row + lax.rem(base + 2 * j, 2 * NX)
@@ -84,10 +86,13 @@
 
     barrier = pltpu.get_barrier_semaphore()
     greeted = [(i, peer(d)) for d in range(1, ND)]
-    greeted += [(c, me) for c in (partner, up, down, chip(1), chip(2), chip(3))]
+    greeted += [(c, me) for c in (partner, chip(1), chip(2), chip(3))]
     for who in greeted:
         pl.semaphore_signal(barrier, inc=1, device_id=who, device_id_type=MESH)
-    pl.semaphore_wait(barrier, len(greeted))
+    pl.when(not_first)(
+        lambda: pl.semaphore_signal(barrier, inc=1, device_id=(down, me), device_id_type=MESH)
+    )
+    pl.semaphore_wait(barrier, len(greeted) + jnp.where(not_last, 1, 0))
 
     spread = [[], []]
     for half in (0, 1):
@@ -98,6 +103,14 @@
             )
             copy.start()
             spread[half].append(copy)
+
+    @pl.when(jnp.logical_not(not_first))
+    def _():
+        kv[8] = jnp.zeros((2 * T, D), bf16)
+
+    @pl.when(jnp.logical_not(not_last))
+    def _():
+        zst[...] = jnp.zeros(zst.shape, bf16)
 
     lo, hi = doc_rows(lens_ref)
     pos0 = (i * T).astype(f32)
@@ -137,7 +150,7 @@
         loads[2 + half].wait()
         for copy in spread[half]:
             copy.wait()
-        zcopy(half).start()
+        pl.when(not_last)(zcopy(half).start)
         for j in (1, 3, 2):
             pl.when(x + j < NX)(xcopy(j, half).start)
         pl.when(core == 0)(lambda half=half: share(0, half).start())
@@ -160,7 +173,7 @@
 
     scores(0)
     for half in (0, 1):
-        zcopy(half).wait_recv()
+        pl.when(not_first)(zcopy(half).wait_recv)
         for j in (1, 3, 2):
             pl.when(x + j >= NX)(xcopy(j, half).start)
         pl.when(core == 1)(lambda half=half: share(3, half).start())
@@ -177,7 +190,7 @@
     for m in range(4):
         share(m, 1).wait()
     for half in (0, 1):
-        zcopy(half).wait_send()
+        pl.when(not_last)(zcopy(half).wait_send)
         for j in (1, 3, 2):
             xcopy(j, half).wait_send()
     for j in range(W):
@@ -207,10 +220,13 @@
         d3 = r1 - d2
         dall[cols] = jnp.where(lane == 0, d1, jnp.where(lane == 1, d2, jnp.where(lane == 2, d3, 0.0))).astype(bf16)
 
-    def gradients(j):
+    def value_gradient(j):
+        rows = slice(j * T, (j + 1) * T)
+        return jnp.dot(p_ref[rows], g2all[...], preferred_element_type=f32) * (1.0 / SCALE)
+
+    def key_gradient(j):
         rows = slice(j * T, (j + 1) * T)
         left = jnp.concatenate([kv[j, VALUES], three[...]], axis=1)
-        dv = jnp.dot(p_ref[rows], g2all[...], preferred_element_type=f32)
         dk = None
         for part in range(2):
             for h in range(part * H // 2, (part + 1) * H // 2):
@@ -221,15 +237,20 @@
             cols = slice(part * H // 2 * T, (part + 1) * H // 2 * T)
             piece = jnp.dot(ds_ref[rows, cols], qall[cols], preferred_element_type=f32)
             dk = piece if dk is None else dk + piece
-        return dk, dv * (1.0 / SCALE)
+        return dk
+
+    gradient = (key_gradient, value_gradient)
 
     def query_gradient(h):
         cols = slice(h * T, (h + 1) * T)
         dqt = jnp.dot(kT[...], ds_ref[:, cols], preferred_element_type=f32)
         dq_ref[:, h * D : (h + 1) * D] = jnp.transpose(dqt).astype(bf16)
 
-    def give(m):
-        return remote(gb.at[2 * m + 1], pst.at[m], psend.at[2, m], precv.at[2, m], (partner, me))
+    def give(m, half):
+        part = half_of[half]
+        return remote(
+            gb.at[2 * m + 1, part], pst.at[m, part], psend.at[2 + half, m], precv.at[2 + half, m], (partner, me)
+        )
 
     def xback(j, half):
         part = half_of[half]
@@ -241,54 +262,42 @@
         part = half_of[half]
         return remote(gb.at[8, part], zst.at[part], zsend.at[2 + half], zrecv.at[2 + half], (down, me))
 
-    own = None
-    for j in ORDER:
-        dk, dv = gradients(j)
-        if j == 0:
-            own = [dk, dv]
-        elif j % 2:
-            gb[j, KEYS] = dk.astype(bf16)
-            gb[j, VALUES] = dv.astype(bf16)
-            give(j // 2).start()
-        else:
-            if j == 6:
-                give(3).wait()
-                give(2).wait()
-            elif j == 4:
-                give(1).wait()
-            else:
-                give(0).wait()
-            other = pst[j // 2 - core].astype(f32)
-            gb[j, KEYS] = (dk + other[:T]).astype(bf16)
-            gb[j, VALUES] = (dv + other[T:]).astype(bf16)
-            for half in (0, 1):
-                xback(j // 2, half).start()
+    def odd(j, half):
+        gb[j, half_of[half]] = gradient[half](j).astype(bf16)
+        give(j // 2, half).start()
+
+    def even(j, half):
+        part = half_of[half]
+        grad = gradient[half](j)
+        for m in {6: (3, 2), 4: (1,), 2: (0,)}[j]:
+            give(m, half).wait()
+        gb[j, part] = (grad + pst[j // 2 - core, part].astype(f32)).astype(bf16)
+        xback(j // 2, half).start()
 
     first_part = jnp.where(core == 0, 1.0, 0.0)
     last_part = jnp.where(core == 1, 1.0, 0.0)
-    for h in range(3):
-        query_gradient(h)
-    prev = [None, None]
-    for half in (0, 1):
-        part = half_of[half]
-        own[half] += pst[0, part].astype(f32) * first_part
-        prev[half] = pst[3, part].astype(f32) * last_part
+
+    def fold(half):
+        part = half_of[half]
+        total = own[part] + pst[0, part].astype(f32) * first_part
+        prev = pst[3, part].astype(f32) * last_part
         for j in (3, 2, 1):
             xback(j, half).wait()
             mine = jnp.where(x + j < NX, 1.0, 0.0)
             got = xst[j, part].astype(f32)
-            own[half] += got * mine
-            prev[half] += got * (1.0 - mine)
-        gb[8, part] = prev[half].astype(bf16)
-        zback(half).start()
-    for h in range(3, 6):
-        query_gradient(h)
+            total += got * mine
+            prev += got * (1.0 - mine)
+        gb[8, part] = prev.astype(bf16)
+        pl.when(not_first)(zback(half).start)
+        own[part] = total
+
     out = (kg, vg)
     last = []
-    for half in (0, 1):
-        part = half_of[half]
-        zback(half).wait()
-        fin[part] = (own[half] + zst[part].astype(f32)).astype(bf16)
+
+    def finish(half):
+        part = half_of[half]
+        pl.when(not_last)(zback(half).wait_recv)
+        fin[part] = (own[part] + zst[part].astype(f32)).astype(bf16)
         for d in range(1, ND):
             rows = pl.ds(pl.multiple_of(half * T + peer(d) * ROWS, ROWS), ROWS)
             copy = remote(
@@ -296,10 +305,32 @@
             )
             copy.start()
             last.append(copy)
+
+    for j in (7, 5, 3, 1):
+        odd(j, 1)
+    for j in (6, 4, 2):
+        even(j, 1)
+    own[VALUES] = value_gradient(0)
+    for j in (7, 5, 3, 1):
+        odd(j, 0)
+    even(6, 0)
+    fold(1)
+    for j in (4, 2):
+        even(j, 0)
+    own[KEYS] = key_gradient(0)
+    for h in range(4):
+        query_gradient(h)
+    finish(1)
+    for h in range(4, 6):
+        query_gradient(h)
+    fold(0)
     for h in range(6, 8):
         query_gradient(h)
+    finish(0)
     kg[:, own_col] = fin[own_row[0]]
     vg[:, own_col] = fin[own_row[1]]
+    for half in (0, 1):
+        pl.when(not_first)(zback(half).wait_send)
     for copy in last:
         copy.wait()
     dk_ref[...] = kg[...]
@@ -339,6 +370,7 @@
             vmem((4, 2 * T, D), bf16),
             vmem((4, 2 * T, D), bf16),
             vmem((2 * T, D), bf16),
+            vmem((2 * T, D), f32),
             vmem((2 * T, D), bf16),
             vmem((ROWS, ND * D), bf16),
             vmem((ROWS, ND * D), bf16),
@@ -361,8 +393,8 @@
             dma((4,)),
             dma((4, NX)),
             dma((4, NX)),
-            dma((3, 4)),
-            dma((3, 4)),
+            dma((4, 4)),
+            dma((4, 4)),
         ],
         compiler_params=pltpu.CompilerParams(
             collective_id=0, has_side_effects=True, vmem_limit_bytes=52 << 20

time: 62.1 us -> 56.1 us (0.903)
  the two profiles are of different devices: /device:TPU:6 before, /device:TPU:128 now
where the time goes in v3:
time: 56.1 us; the launch traced here: 55.9 us
  Pallas kernels  54.4 us (97%)
  between operations  0.81 us (1%)
  local copies, waits for them, and re-layouts  0.65 us (1%)
    pallas_call x1, Pallas kernels, body(): pl.pallas_call(functools.partial(kernel, lax.axis_size('ctx')), out_shape...  53.4 us

profile of v3, /device:TPU:128, one launch (start us, length us, event | category | flops | bytes accessed | tf_op | source)
XLA Modules:
  0.0 55.9 jit_solution(87833194022473332)
XLA Ops:
  0.6 0.0 copy-start
  0.6 0.6 %copy-done = s32[32]{0:T(128)S(1)} copy-done((s32[32]{0:T(128)S(1)}, s32[32]{0:T(128)}, u32[]{:S(2)}) %copy-start) | copy-done | bytes 152
  1.3 53.4 %attention.1 = (bf16[256,1024]{1,0:T(8,128)(2,1)S(1)}, bf16[256,1024]{1,0:T(8,128)(2,1)S(1)}, bf16[32,1024]{1,0:T(8,128)(2,1)S(1)}, bf16[32,1024]{1,0:T(8,128)(2,1)S(1)}) custom-call(s32[1,32]{1,0:T(1,128)S(1)} %bitcast.1, bf16[256,1024]{1,0:T(8,128)(2,1)} %q_hbm.1, bf16[256,1024]{1,0:T(8,128)(2,1)} %g_hbm.1, bf16[32,1024]{1,0:T(8,128)(2,1)} %k_hbm.1, ...), custom_call_target="tpu_custom_call" | custom-call | tf_op jit(solution)/shard_map/attention/pallas_call | solution.py:360
  54.7 1.0 %write.1 = (bf16[256,1024]{1,0:T(8,128)(2,1)}, bf16[256,1024]{1,0:T(8,128)(2,1)}, bf16[32,1024]{1,0:T(8,128)(2,1)}, bf16[32,1024]{1,0:T(8,128)(2,1)}) custom-call(bf16[256,1024]{1,0:T(8,128)(2,1)S(1)} %get-tuple-element.8.o_in, bf16[256,1024]{1,0:T(8,128)(2,1)S(1)} %get-tuple-element.9.dq_in, bf16[32,1024]{1,0:T(8,128)(2,1)S(1)} %get-tuple-element.10.dk_in, ...), custom_call_target="tpu_custom_call" | custom-call | tf_op jit(solution)/shard_map/write/pallas_call | solution.py:404
Async XLA Ops:
  0.6 0.7 %copy-start = (s32[32]{0:T(128)S(1)}, s32[32]{0:T(128)}, u32[]{:S(2)}) copy-start(s32[32]{0:T(128)} %param.9) | copy-start | bytes 388

commit v4 on v3

--- a/solution.py
+++ b/solution.py
@@ -44,8 +44,8 @@
 
 
 def kernel(
-    nctx, lens_ref, q_hbm, g_hbm, k_hbm, v_hbm, o_ref, dq_ref, dk_ref, dv_ref,
-    q_ref, g_ref, kv, gb, pst, xst, zst, own, fin, kg, vg,
+    nctx, lens_hbm, q_hbm, g_hbm, k_hbm, v_hbm, o_ref, dq_ref, dk_ref, dv_ref,
+    lens_ref, q_ref, g_ref, kv, gb, pst, xst, zst, own, fin, kg, vg,
     qa, kb, three, qall, g2all, dall, kT, vT, m_ref, s_ref, p_ref, ds_ref,
     lsem, asend, arecv, zsend, zrecv, xsend, xrecv, psend, precv,
 ):
@@ -81,6 +81,7 @@
         loads.append(
             pltpu.make_async_copy(source[half].at[:, own_col], kv.at[0, own_row[half]], lsem.at[2 + half])
         )
+    loads.append(pltpu.make_async_copy(lens_hbm, lens_ref, lsem.at[4]))
     for copy in loads:
         copy.start()
 
@@ -112,6 +113,7 @@
     def _():
         zst[...] = jnp.zeros(zst.shape, bf16)
 
+    loads[4].wait()
     lo, hi = doc_rows(lens_ref)
     pos0 = (i * T).astype(f32)
     sub = lax.broadcasted_iota(jnp.int32, (T, D), 0).astype(f32)
@@ -196,17 +198,19 @@
     for j in range(W):
         vT[:D, j * T : (j + 1) * T] = jnp.transpose(kv[j, VALUES])
 
-    for h in range(H):
+    def weigh(h):
+        cols = slice(h * T, (h + 1) * T)
+        top = jnp.max(m_ref[:, cols], axis=0, keepdims=True)
+        for j in range(W):
+            rows = slice(j * T, (j + 1) * T)
+            p_ref[rows, cols] = jnp.exp2((s_ref[rows, cols] - top) * C2).astype(bf16)
+
+    def attend(h):
         cols = slice(h * T, (h + 1) * T)
         col = slice(h * D, (h + 1) * D)
-        mc = jnp.max(m_ref[:, cols], axis=0, keepdims=True) * C2
-        for j in range(W):
-            rows = slice(j * T, (j + 1) * T)
-            p_ref[rows, cols] = jnp.exp2(s_ref[rows, cols] * C2 - mc).astype(bf16)
         ot = jnp.dot(vT[...], p_ref[:, cols], preferred_element_type=f32)
         o = jnp.transpose(ot[:D])
-        total = jnp.transpose(ot[D : D + 8])[:, 0:1]
-        inv = 1.0 / total
+        inv = jnp.transpose(1.0 / ot[D : D + 8])[:, 0:1]
         ob = (o * inv).astype(bf16)
         o_ref[:, col] = ob
         gf = g_ref[:, col].astype(f32)
@@ -219,6 +223,16 @@
         d2 = r1.astype(bf16).astype(f32)
         d3 = r1 - d2
         dall[cols] = jnp.where(lane == 0, d1, jnp.where(lane == 1, d2, jnp.where(lane == 2, d3, 0.0))).astype(bf16)
+
+    for stage in range(0, H + 2, 2):
+
+        @pl.when(i >= 0)
+        def _(stage=stage):
+            for h in (stage, stage + 1):
+                if h < H:
+                    weigh(h)
+                if h >= 2:
+                    attend(h - 2)
 
     def value_gradient(j):
         rows = slice(j * T, (j + 1) * T)
@@ -252,15 +266,17 @@
             gb.at[2 * m + 1, part], pst.at[m, part], psend.at[2 + half, m], precv.at[2 + half, m], (partner, me)
         )
 
-    def xback(j, half):
-        part = half_of[half]
+    quarter_of = [slice(e * T // 2, (e + 1) * T // 2) for e in range(4)]
+
+    def xback(j, e):
+        part = quarter_of[e]
         return remote(
-            gb.at[2 * j, part], xst.at[j, part], xsend.at[2 + half, j], xrecv.at[2 + half, j], (chip(NX - j), me)
-        )
-
-    def zback(half):
-        part = half_of[half]
-        return remote(gb.at[8, part], zst.at[part], zsend.at[2 + half], zrecv.at[2 + half], (down, me))
+            gb.at[2 * j, part], xst.at[j, part], xsend.at[2 + e, j], xrecv.at[2 + e, j], (chip(NX - j), me)
+        )
+
+    def zback(e):
+        part = quarter_of[e]
+        return remote(gb.at[8, part], zst.at[part], zsend.at[2 + e], zrecv.at[2 + e], (down, me))
 
     def odd(j, half):
         gb[j, half_of[half]] = gradient[half](j).astype(bf16)
@@ -272,39 +288,42 @@
         for m in {6: (3, 2), 4: (1,), 2: (0,)}[j]:
             give(m, half).wait()
         gb[j, part] = (grad + pst[j // 2 - core, part].astype(f32)).astype(bf16)
-        xback(j // 2, half).start()
+        for e in (2 * half, 2 * half + 1):
+            xback(j // 2, e).start()
 
     first_part = jnp.where(core == 0, 1.0, 0.0)
     last_part = jnp.where(core == 1, 1.0, 0.0)
 
-    def fold(half):
-        part = half_of[half]
+    def fold(e):
+        part = quarter_of[e]
         total = own[part] + pst[0, part].astype(f32) * first_part
         prev = pst[3, part].astype(f32) * last_part
         for j in (3, 2, 1):
-            xback(j, half).wait()
+            xback(j, e).wait()
             mine = jnp.where(x + j < NX, 1.0, 0.0)
             got = xst[j, part].astype(f32)
             total += got * mine
             prev += got * (1.0 - mine)
         gb[8, part] = prev.astype(bf16)
-        pl.when(not_first)(zback(half).start)
+        pl.when(not_first)(zback(e).start)
         own[part] = total
 
     out = (kg, vg)
-    last = []
-
-    def finish(half):
-        part = half_of[half]
-        pl.when(not_last)(zback(half).wait_recv)
+
+    def deliver(half, d):
+        rows = pl.ds(pl.multiple_of(half * T + peer(d) * ROWS, ROWS), ROWS)
+        return remote(
+            fin.at[rows], out[half].at[:, own_col], asend.at[2 + half, d], arecv.at[2 + half, d], (i, peer(d))
+        )
+
+    def finish(e):
+        part = quarter_of[e]
+        half = e // 2
+        pl.when(not_last)(zback(e).wait_recv)
         fin[part] = (own[part] + zst[part].astype(f32)).astype(bf16)
         for d in range(1, ND):
-            rows = pl.ds(pl.multiple_of(half * T + peer(d) * ROWS, ROWS), ROWS)
-            copy = remote(
-                fin.at[rows], out[half].at[:, own_col], asend.at[2 + half, d], arecv.at[2 + half, d], (i, peer(d))
-            )
-            copy.start()
-            last.append(copy)
+            here = lax.div(peer(d), ND // 2) == e % 2
+            pl.when(here)(deliver(half, d).start)
 
     for j in (7, 5, 3, 1):
         odd(j, 1)
@@ -314,25 +333,30 @@
     for j in (7, 5, 3, 1):
         odd(j, 0)
     even(6, 0)
-    fold(1)
+    fold(2)
+    fold(3)
     for j in (4, 2):
         even(j, 0)
     own[KEYS] = key_gradient(0)
     for h in range(4):
         query_gradient(h)
-    finish(1)
+    finish(2)
+    finish(3)
     for h in range(4, 6):
         query_gradient(h)
     fold(0)
+    fold(1)
     for h in range(6, 8):
         query_gradient(h)
     finish(0)
+    finish(1)
     kg[:, own_col] = fin[own_row[0]]
     vg[:, own_col] = fin[own_row[1]]
-    for half in (0, 1):
-        pl.when(not_first)(zback(half).wait_send)
-    for copy in last:
-        copy.wait()
+    for e in range(4):
+        pl.when(not_first)(zback(e).wait_send)
+    for half in (1, 0):
+        for d in range(1, ND):
+            deliver(half, d).wait()
     dk_ref[...] = kg[...]
     dv_ref[...] = vg[...]
 
@@ -355,14 +379,15 @@
     small = jax.ShapeDtypeStruct((ROWS, ND * D), bf16)
     arrays = [
         pltpu.with_memory_space_constraint(a, pltpu.HBM)
-        for a in (queries, output_gradient, key_vectors, value_vectors)
+        for a in (doc_lengths.reshape(1, -1), queries, output_gradient, key_vectors, value_vectors)
     ]
     parts = pl.pallas_call(
         functools.partial(kernel, lax.axis_size("ctx")),
         out_shape=(big, big, small, small),
-        in_specs=[vm] + [free] * 4,
+        in_specs=[free] * 5,
         out_specs=(vm,) * 4,
         scratch_shapes=[
+            vmem((1, doc_lengths.shape[0]), jnp.int32),
             vmem((T, H * D), bf16),
             vmem((T, H * D), bf16),
             vmem((9, 2 * T, D), bf16),
@@ -386,13 +411,13 @@
             vmem((W * T, H * T), f32),
             vmem((W * T, H * T), bf16),
             vmem((W * T, H * T), bf16),
-            dma((4,)),
+            dma((5,)),
             dma((4, ND)),
             dma((4, ND)),
-            dma((4,)),
-            dma((4,)),
-            dma((4, NX)),
-            dma((4, NX)),
+            dma((6,)),
+            dma((6,)),
+            dma((6, NX)),
+            dma((6, NX)),
             dma((4, 4)),
             dma((4, 4)),
         ],
@@ -400,7 +425,7 @@
             collective_id=0, has_side_effects=True, vmem_limit_bytes=52 << 20
         ),
         name="attention",
-    )(doc_lengths.reshape(1, -1), *arrays)
+    )(*arrays)
     return pl.pallas_call(
         write_kernel,
         out_shape=(big, big, small, small),

time: 56.1 us -> 54.4 us (0.970)
  Pallas kernels: 54.4 us -> 53.5 us
  local copies, waits for them, and re-layouts: 0.65 us -> 0 us
    pallas_call x1, Pallas kernels: 53.4 us -> 52.5 us  [body(): pl.pallas_call(functools.partial(kernel, lax.axis_size('ctx')), out_shape...]
    unnamed x2 -> x0, local copies, waits for them, and re-layouts: 0.65 us -> none
where the time goes in v4:
time: 54.4 us; the launch traced here: 54.3 us
  Pallas kernels  53.5 us (98%)
  between operations  0.8 us (1%)
    pallas_call x1, Pallas kernels, body(): pl.pallas_call(functools.partial(kernel, lax.axis_size('ctx')), out_shape...  52.5 us

profile of v4, /device:TPU:128, one launch (start us, length us, event | category | flops | bytes accessed | tf_op | source)
XLA Modules:
  0.0 54.3 jit_solution(17293597647583019219)
XLA Ops:
  0.6 52.5 %attention.1 = (bf16[256,1024]{1,0:T(8,128)(2,1)S(1)}, bf16[256,1024]{1,0:T(8,128)(2,1)S(1)}, bf16[32,1024]{1,0:T(8,128)(2,1)S(1)}, bf16[32,1024]{1,0:T(8,128)(2,1)S(1)}) custom-call(s32[1,32]{1,0:T(1,128)} %bitcast.1, bf16[256,1024]{1,0:T(8,128)(2,1)} %q_hbm.1, bf16[256,1024]{1,0:T(8,128)(2,1)} %g_hbm.1, bf16[32,1024]{1,0:T(8,128)(2,1)} %k_hbm.1, ...), custom_call_target="tpu_custom_call" | custom-call | tf_op jit(solution)/shard_map/attention/pallas_call | solution.py:384
  53.1 1.0 %write.1 = (bf16[256,1024]{1,0:T(8,128)(2,1)}, bf16[256,1024]{1,0:T(8,128)(2,1)}, bf16[32,1024]{1,0:T(8,128)(2,1)}, bf16[32,1024]{1,0:T(8,128)(2,1)}) custom-call(bf16[256,1024]{1,0:T(8,128)(2,1)S(1)} %get-tuple-element.8.o_in, bf16[256,1024]{1,0:T(8,128)(2,1)S(1)} %get-tuple-element.9.dq_in, bf16[32,1024]{1,0:T(8,128)(2,1)S(1)} %get-tuple-element.10.dk_in, ...), custom_call_target="tpu_custom_call" | custom-call | tf_op jit(solution)/shard_map/write/pallas_call | solution.py:429

commit v5 on v4

--- a/solution.py
+++ b/solution.py
@@ -183,20 +183,15 @@
         xcopy(j, 0).wait_recv()
         share(j - core, 0).start()
         scores(2 * j)
+    for m in (0, 1):
+        share(m, 0).wait()
+        scores(2 * m + 1)
     for j in (1, 3, 2):
         xcopy(j, 1).wait_recv()
         share(j - core, 1).start()
-    for m in range(4):
+    for m in (2, 3):
         share(m, 0).wait()
         scores(2 * m + 1)
-    for m in range(4):
-        share(m, 1).wait()
-    for half in (0, 1):
-        pl.when(not_last)(zcopy(half).wait_send)
-        for j in (1, 3, 2):
-            xcopy(j, half).wait_send()
-    for j in range(W):
-        vT[:D, j * T : (j + 1) * T] = jnp.transpose(kv[j, VALUES])
 
     def weigh(h):
         cols = slice(h * T, (h + 1) * T)
@@ -225,6 +220,11 @@
         dall[cols] = jnp.where(lane == 0, d1, jnp.where(lane == 1, d2, jnp.where(lane == 2, d3, 0.0))).astype(bf16)
 
     for stage in range(0, H + 2, 2):
+        if stage == 2:
+            for m in range(4):
+                share(m, 1).wait()
+            for j in range(W):
+                vT[:D, j * T : (j + 1) * T] = jnp.transpose(kv[j, VALUES])
 
         @pl.when(i >= 0)
         def _(stage=stage):
@@ -285,7 +285,7 @@
     def even(j, half):
         part = half_of[half]
         grad = gradient[half](j)
-        for m in {6: (3, 2), 4: (1,), 2: (0,)}[j]:
+        for m in {4: (2, 1), 6: (3,), 2: (0,)}[j]:
             give(m, half).wait()
         gb[j, part] = (grad + pst[j // 2 - core, part].astype(f32)).astype(bf16)
         for e in (2 * half, 2 * half + 1):
@@ -298,7 +298,7 @@
         part = quarter_of[e]
         total = own[part] + pst[0, part].astype(f32) * first_part
         prev = pst[3, part].astype(f32) * last_part
-        for j in (3, 2, 1):
+        for j in (2, 3, 1):
             xback(j, e).wait()
             mine = jnp.where(x + j < NX, 1.0, 0.0)
             got = xst[j, part].astype(f32)
@@ -325,28 +325,28 @@
             here = lax.div(peer(d), ND // 2) == e % 2
             pl.when(here)(deliver(half, d).start)
 
-    for j in (7, 5, 3, 1):
+    for j in (5, 3, 7, 1):
         odd(j, 1)
-    for j in (6, 4, 2):
+    for j in (4, 6, 2):
         even(j, 1)
     own[VALUES] = value_gradient(0)
-    for j in (7, 5, 3, 1):
-        odd(j, 0)
+    odd(5, 0)
+    odd(3, 0)
+    odd(7, 0)
+    even(4, 0)
+    odd(1, 0)
     even(6, 0)
     fold(2)
     fold(3)
-    for j in (4, 2):
-        even(j, 0)
+    even(2, 0)
     own[KEYS] = key_gradient(0)
     for h in range(4):
         query_gradient(h)
+    fold(0)
+    fold(1)
     finish(2)
     finish(3)
-    for h in range(4, 6):
-        query_gradient(h)
-    fold(0)
-    fold(1)
-    for h in range(6, 8):
+    for h in range(4, 8):
         query_gradient(h)
     finish(0)
     finish(1)
@@ -354,6 +354,10 @@
     vg[:, own_col] = fin[own_row[1]]
     for e in range(4):
         pl.when(not_first)(zback(e).wait_send)
+    for half in (0, 1):
+        pl.when(not_last)(zcopy(half).wait_send)
+        for j in (1, 3, 2):
+            xcopy(j, half).wait_send()
     for half in (1, 0):
         for d in range(1, ND):
             deliver(half, d).wait()

time: 54.4 us -> 53.4 us (0.982)
  the two profiles are of different devices: /device:TPU:128 before, /device:TPU:6 now
where the time goes in v5:
time: 53.4 us; the launch traced here: 52.8 us
  Pallas kernels  52 us (97%)
  between operations  0.8 us (1%)
    pallas_call x1, Pallas kernels, body(): pl.pallas_call(functools.partial(kernel, lax.axis_size('ctx')), out_shape...  51 us

profile of v5, /device:TPU:6, one launch (start us, length us, event | category | flops | bytes accessed | tf_op | source)
XLA Modules:
  0.0 52.8 jit_solution(1807356472132866415)
XLA Ops:
  0.6 51.0 %attention.1 = (bf16[256,1024]{1,0:T(8,128)(2,1)S(1)}, bf16[256,1024]{1,0:T(8,128)(2,1)S(1)}, bf16[32,1024]{1,0:T(8,128)(2,1)S(1)}, bf16[32,1024]{1,0:T(8,128)(2,1)S(1)}) custom-call(s32[1,32]{1,0:T(1,128)} %bitcast.1, bf16[256,1024]{1,0:T(8,128)(2,1)} %q_hbm.1, bf16[256,1024]{1,0:T(8,128)(2,1)} %g_hbm.1, bf16[32,1024]{1,0:T(8,128)(2,1)} %k_hbm.1, ...), custom_call_target="tpu_custom_call" | custom-call | tf_op jit(solution)/shard_map/attention/pallas_call | solution.py:388
  51.6 1.0 %write.1 = (bf16[256,1024]{1,0:T(8,128)(2,1)}, bf16[256,1024]{1,0:T(8,128)(2,1)}, bf16[32,1024]{1,0:T(8,128)(2,1)}, bf16[32,1024]{1,0:T(8,128)(2,1)}) custom-call(bf16[256,1024]{1,0:T(8,128)(2,1)S(1)} %get-tuple-element.8.o_in, bf16[256,1024]{1,0:T(8,128)(2,1)S(1)} %get-tuple-element.9.dq_in, bf16[32,1024]{1,0:T(8,128)(2,1)S(1)} %get-tuple-element.10.dk_in, ...), custom_call_target="tpu_custom_call" | custom-call | tf_op jit(solution)/shard_map/write/pallas_call | solution.py:433

commit v6 on v5

--- a/solution.py
+++ b/solution.py
@@ -183,15 +183,20 @@
         xcopy(j, 0).wait_recv()
         share(j - core, 0).start()
         scores(2 * j)
-    for m in (0, 1):
-        share(m, 0).wait()
-        scores(2 * m + 1)
     for j in (1, 3, 2):
         xcopy(j, 1).wait_recv()
         share(j - core, 1).start()
-    for m in (2, 3):
+    for m in range(4):
         share(m, 0).wait()
         scores(2 * m + 1)
+    for m in range(4):
+        share(m, 1).wait()
+    for half in (0, 1):
+        pl.when(not_last)(zcopy(half).wait_send)
+        for j in (1, 3, 2):
+            xcopy(j, half).wait_send()
+    for j in range(W):
+        vT[:D, j * T : (j + 1) * T] = jnp.transpose(kv[j, VALUES])
 
     def weigh(h):
         cols = slice(h * T, (h + 1) * T)
@@ -220,11 +225,6 @@
         dall[cols] = jnp.where(lane == 0, d1, jnp.where(lane == 1, d2, jnp.where(lane == 2, d3, 0.0))).astype(bf16)
 
     for stage in range(0, H + 2, 2):
-        if stage == 2:
-            for m in range(4):
-                share(m, 1).wait()
-            for j in range(W):
-                vT[:D, j * T : (j + 1) * T] = jnp.transpose(kv[j, VALUES])
 
         @pl.when(i >= 0)
         def _(stage=stage):
@@ -354,10 +354,6 @@
     vg[:, own_col] = fin[own_row[1]]
     for e in range(4):
         pl.when(not_first)(zback(e).wait_send)
-    for half in (0, 1):
-        pl.when(not_last)(zcopy(half).wait_send)
-        for j in (1, 3, 2):
-            xcopy(j, half).wait_send()
     for half in (1, 0):
         for d in range(1, ND):
             deliver(half, d).wait()

time: 53.4 us -> 53.2 us (level)
  no operation moved by 1% of the time
where the time goes in v6:
time: 53.2 us; the launch traced here: 52.6 us
  Pallas kernels  51.8 us (97%)
  between operations  0.8 us (2%)
    pallas_call x1, Pallas kernels, body(): pl.pallas_call(functools.partial(kernel, lax.axis_size('ctx')), out_shape...  50.7 us

profile of v6, /device:TPU:6, one launch (start us, length us, event | category | flops | bytes accessed | tf_op | source)
XLA Modules:
  0.0 52.6 jit_solution(1178974393737905174)
XLA Ops:
  0.6 50.7 %attention.1 = (bf16[256,1024]{1,0:T(8,128)(2,1)S(1)}, bf16[256,1024]{1,0:T(8,128)(2,1)S(1)}, bf16[32,1024]{1,0:T(8,128)(2,1)S(1)}, bf16[32,1024]{1,0:T(8,128)(2,1)S(1)}) custom-call(s32[1,32]{1,0:T(1,128)} %bitcast.1, bf16[256,1024]{1,0:T(8,128)(2,1)} %q_hbm.1, bf16[256,1024]{1,0:T(8,128)(2,1)} %g_hbm.1, bf16[32,1024]{1,0:T(8,128)(2,1)} %k_hbm.1, ...), custom_call_target="tpu_custom_call" | custom-call | tf_op jit(solution)/shard_map/attention/pallas_call | solution.py:384
  51.4 1.0 %write.1 = (bf16[256,1024]{1,0:T(8,128)(2,1)}, bf16[256,1024]{1,0:T(8,128)(2,1)}, bf16[32,1024]{1,0:T(8,128)(2,1)}, bf16[32,1024]{1,0:T(8,128)(2,1)}) custom-call(bf16[256,1024]{1,0:T(8,128)(2,1)S(1)} %get-tuple-element.8.o_in, bf16[256,1024]{1,0:T(8,128)(2,1)S(1)} %get-tuple-element.9.dq_in, bf16[32,1024]{1,0:T(8,128)(2,1)S(1)} %get-tuple-element.10.dk_in, ...), custom_call_target="tpu_custom_call" | custom-call | tf_op jit(solution)/shard_map/write/pallas_call | solution.py:429
